TPU v7x, 256 devices: a whole 4x4x8 slice. The times are simulated.
256 devices in a mesh: seq: 32 (over z_hi, x, core), fsdp: 8 (over z_lo, y).
Axes of the slice: x: 4, y: 4, z: 8 (z_hi: 4, z_lo: 2; z = z_hi * 2 + z_lo), core: 2. Of those that a mesh axis runs over, the one named last changes fastest.
Arguments:
- inputs: bfloat16 [8, 128, 32, 4096], P('fsdp', None, 'seq'), may hold values from -6 to 6
- queries: bfloat16 [8, 128, 32, 4096], P('fsdp', None, 'seq'), may hold values from -1000 to 1000
- rotated_keys: bfloat16 [8, 128, 32, 512], P('fsdp', None, 'seq'), may hold values from -6 to 6
- out_grad: bfloat16 [8, 128, 32, 4096], P('fsdp', None, 'seq'), may hold values from -6 to 6
- value_weight: bfloat16 [4096, 512], P(('seq', 'fsdp')), may hold values from -0.09375 to 0.09375
- fisher: float32 [4096, 512], P(('seq', 'fsdp')), may hold values from 0.2 to 20
- anchor: float32 [4096, 512], P(('seq', 'fsdp')), may hold values from -0.25 to 0.25
- doc_starts: int32 [8, 64], P('fsdp'), may hold values from 0 to 4064, as said below
- owners: int32 [8, 64], P('fsdp'), may hold values from 0 to 31, as said below
Outputs:
- query_grad: bfloat16 [8, 32, 6, 32, 4096], P('fsdp', 'seq')
- key_grad: bfloat16 [8, 128, 32, 512], P('fsdp', None, 'seq')
- input_grad: bfloat16 [8, 128, 32, 4096], P('fsdp', None, 'seq')
- ewc_grad: float32 [4096, 512], P(('seq', 'fsdp'))
Inputs may be any that keep to these rules, and one draw needn't show every extreme that they name: `doc_starts`: in each sequence the starts rise strictly from 0; every document's length (4096 minus the last start for the last one) is a multiple of 32. Each of the 32 owners is named by exactly two documents of a sequence; one owner's documents hold at most 192 positions in all, and in every sequence some owner holds exactly that many.
All inputs are finite; a program needn't handle non-finite values.
Results may differ from a plain program's by a relative error of at most 0.029.
Values may be sent and summed in bfloat16 or wider, within the bound.
No kernel may reach another device: no remote copies, remote signals or barrier semaphores. Data moves between devices by JAX's collectives and lax.ppermute only.
A program may use at most 128 MiB of HBM per device.

v0:
```python
import math

import jax
import jax.numpy as jnp
from jax import lax
from jax.sharding import PartitionSpec as P

KVH = 4
HD = 128


SCORE_NEG = -1e30
EWC_LAMBDA = 4.0


def round_plan(starts, owner_list, lane_count, rounds):
    round_ids = jnp.arange(rounds, dtype=jnp.int32)
    start_rounds = starts // lane_count
    doc_of = jnp.sum((start_rounds[None, :] <= round_ids[:, None]).astype(jnp.int32), axis=1) - 1
    doc_ids = jnp.arange(starts.shape[0], dtype=jnp.int32)
    onehot = (doc_of[:, None] == doc_ids[None, :]).astype(jnp.int32)
    owner_of = jnp.sum(onehot * owner_list[None, :], axis=1)
    earlier = (owner_of[:, None] == owner_of[None, :]) & (round_ids[None, :] < round_ids[:, None])
    rank_of = jnp.sum(earlier.astype(jnp.int32), axis=1)
    return (doc_of, owner_of, rank_of)


def slot_rounds(owner_of, rank_of, lane_count, capacity):
    lane_ids = jnp.arange(lane_count, dtype=jnp.int32)
    slot_ids = jnp.arange(capacity, dtype=jnp.int32)
    round_ids = jnp.arange(owner_of.shape[0], dtype=jnp.int32)
    match = (owner_of[None, None, :] == lane_ids[None, :, None]) & (
        rank_of[None, None, :] == slot_ids[:, None, None]
    )
    source = jnp.sum(match.astype(jnp.int32) * round_ids[None, None, :], axis=2)
    filled = jnp.any(match, axis=2)
    return (source, filled)


def attend(query_in, grad_in, key_in, value_in, visible):
    slot_count = query_in.shape[0] * query_in.shape[1]
    group = query_in.shape[3] // HD
    scale = 1.0 / math.sqrt(HD)
    query_parts = []
    key_parts = []
    value_parts = []
    for item_index in range(query_in.shape[2]):
        q_item = query_in[:, :, item_index, :].reshape(slot_count, group, HD)
        g_item = grad_in[:, :, item_index, :].reshape(slot_count, group, HD)
        k_item = key_in[:, :, item_index, :].reshape(slot_count, HD)
        v_item = value_in[:, :, item_index, :].reshape(slot_count, HD)
        scores = (
            jnp.einsum("mgd,kd->gmk", q_item, k_item, preferred_element_type=jnp.float32) * scale
        )
        masked = jnp.where(visible[None], scores, SCORE_NEG)
        peak = jnp.max(masked, axis=2, keepdims=True)
        probs = jnp.where(visible[None], jnp.exp(masked - peak), 0.0)
        totals = jnp.sum(probs, axis=2, keepdims=True)
        probs = probs / jnp.where(totals > 0.0, totals, 1.0)
        probs_b = probs.astype(jnp.bfloat16)
        attn_out = jnp.einsum(
            "gmk,kd->mgd", probs_b, v_item, preferred_element_type=jnp.float32
        ).astype(jnp.bfloat16)
        delta = jnp.einsum("mgd,mgd->gm", g_item, attn_out, preferred_element_type=jnp.float32)
        dprobs = jnp.einsum("mgd,kd->gmk", g_item, v_item, preferred_element_type=jnp.float32)
        dscores = (probs * (dprobs - delta[:, :, None]) * scale).astype(jnp.bfloat16)
        query_grad = jnp.einsum(
            "gmk,kd->mgd", dscores, k_item, preferred_element_type=jnp.float32
        ).astype(jnp.bfloat16)
        key_grad = jnp.einsum(
            "gmk,mgd->kd", dscores, q_item, preferred_element_type=jnp.float32
        ).astype(jnp.bfloat16)
        value_grad = jnp.einsum(
            "gmk,mgd->kd", probs_b, g_item, preferred_element_type=jnp.float32
        ).astype(jnp.bfloat16)
        query_parts.append(query_grad.reshape(query_in.shape[0], query_in.shape[1], group * HD))
        key_parts.append(key_grad.reshape(query_in.shape[0], query_in.shape[1], HD))
        value_parts.append(value_grad.reshape(query_in.shape[0], query_in.shape[1], HD))
    return (
        jnp.stack(query_parts, axis=2),
        jnp.stack(key_parts, axis=2),
        jnp.stack(value_parts, axis=2),
    )


def fetch_weight(value_weight):
    return lax.all_gather(value_weight, ("seq", "fsdp"), axis=0, tiled=True)


def body(inputs, queries, rotated_keys, out_grad, value_weight, fisher, anchor, doc_starts, owners):
    lane_count = lax.axis_size("seq")
    own_lane = lax.axis_index("seq")
    rounds = inputs.shape[1]
    capacity = 3 * rounds // (2 * lane_count)
    token_rows = inputs.reshape(rounds, inputs.shape[3])
    query_rows = queries.reshape(rounds, queries.shape[3])
    key_rows = rotated_keys.reshape(rounds, rotated_keys.shape[3])
    grad_rows = out_grad.reshape(rounds, out_grad.shape[3])
    doc_of, owner_of, rank_of = round_plan(doc_starts[0], owners[0], lane_count, rounds)
    source, filled = slot_rounds(owner_of, rank_of, lane_count, capacity)

    def to_slots(rows):
        picked = jnp.take(rows, source.reshape(-1), axis=0).reshape(capacity, lane_count, KVH, -1)
        return jnp.where(filled[:, :, None, None], picked, jnp.zeros_like(picked))

    query_send = to_slots(query_rows)
    grad_send = to_slots(grad_rows)
    key_send = to_slots(key_rows)
    my_rounds = lax.dynamic_index_in_dim(source, own_lane, 1, keepdims=False)
    my_filled = lax.dynamic_index_in_dim(filled, own_lane, 1, keepdims=False)
    lane_ids = jnp.arange(lane_count, dtype=jnp.int32)
    slot_pos = (my_rounds[:, None] * lane_count + lane_ids[None, :]).reshape(-1)
    round_doc = jnp.where(my_filled, jnp.take(doc_of, my_rounds), -1)
    slot_doc = jnp.broadcast_to(round_doc[:, None], (capacity, lane_count)).reshape(-1)
    slot_live = jnp.broadcast_to(my_filled[:, None], (capacity, lane_count)).reshape(-1)
    visible = (slot_doc[:, None] == slot_doc[None, :]) & (slot_pos[None, :] <= slot_pos[:, None])
    visible = visible & slot_live[:, None] & slot_live[None, :]
    full_weight = fetch_weight(value_weight)
    value_rows = jnp.dot(token_rows, full_weight, preferred_element_type=jnp.float32).astype(
        jnp.bfloat16
    )
    value_send = to_slots(value_rows)
    query_back, key_back, value_back = attend(
        lax.all_to_all(query_send, "seq", split_axis=1, concat_axis=1, tiled=True),
        lax.all_to_all(grad_send, "seq", split_axis=1, concat_axis=1, tiled=True),
        lax.all_to_all(key_send, "seq", split_axis=1, concat_axis=1, tiled=True),
        lax.all_to_all(value_send, "seq", split_axis=1, concat_axis=1, tiled=True),
        visible,
    )
    returned = (
        lax.all_to_all(key_back, "seq", split_axis=1, concat_axis=1, tiled=True),
        lax.all_to_all(value_back, "seq", split_axis=1, concat_axis=1, tiled=True),
    )
    flat_index = rank_of * lane_count + owner_of
    key_home = jnp.take(returned[0].reshape(capacity * lane_count, -1), flat_index, axis=0)
    value_home = jnp.take(returned[1].reshape(capacity * lane_count, -1), flat_index, axis=0)
    input_grad = jnp.einsum(
        "rk,dk->rd", value_home, full_weight, preferred_element_type=jnp.float32
    ).astype(jnp.bfloat16)
    partial_sum = jnp.einsum(
        "rd,rk->dk", token_rows, value_home, preferred_element_type=jnp.float32
    )
    summed = lax.psum_scatter(partial_sum, ("seq", "fsdp"), scatter_dimension=0, tiled=True)
    tokens_total = rounds * lane_count * lax.axis_size("fsdp")
    grad_scale = 1.0 / math.sqrt(tokens_total)
    ewc_grad = summed * grad_scale + EWC_LAMBDA * fisher * (
        value_weight.astype(jnp.float32) - anchor
    )
    query_out = query_back.reshape(1, 1, capacity, lane_count, -1)
    return (
        query_out,
        key_home.reshape(1, rounds, 1, -1),
        input_grad.reshape(1, rounds, 1, -1),
        ewc_grad,
    )


def solution(mesh):
    return jax.shard_map(
        body,
        mesh=mesh,
        in_specs=(
            P("fsdp", None, "seq", None),
            P("fsdp", None, "seq", None),
            P("fsdp", None, "seq", None),
            P("fsdp", None, "seq", None),
            P(("seq", "fsdp"), None),
            P(("seq", "fsdp"), None),
            P(("seq", "fsdp"), None),
            P("fsdp", None),
            P("fsdp", None),
        ),
        out_specs=(
            P("fsdp", "seq", None, None, None),
            P("fsdp", None, "seq", None),
            P("fsdp", None, "seq", None),
            P(("seq", "fsdp"), None),
        ),
        check_vma=False,
    )
```

profile of v0, /device:TPU:0, one launch (start us, length us, event | category | flops | bytes accessed | tf_op | source)
XLA Modules:
  0.0 2143.4 jit_solution(14226648482565059061)
XLA Ops:
  10.8 5.6 gather_fusion.4
  16.4 2.7 gather_fusion.2
  19.1 3.9 broadcast_select_fusion
  23.0 2.9 reshape.287
  25.9 3.9 reshape.283
  29.8 3.6 copy_select_fusion
  33.4 50.5 %all_to_all.30 = bf16[6,32,4,1024]{3,2,0,1:T(4,128)(2,1)} all-to-all(bf16[6,32,4,1024]{3,2,0,1:T(4,128)(2,1)S(1)} %get-tuple-element.56), channel_id=1, replica_groups=mesh['seq'=32,'fsdp'=8] {'seq'}, dimensions={1} | all-to-all | bytes 3145728 | tf_op jit(solution)/shard_map/all_to_all | solution.py:124
  83.9 5.7 all-to-all-start.3
  91.5 1.0 gather_fusion.1
  92.5 0.8 and_and_fusion
  93.2 6.2 fusion.106
  99.7 0.8 copy.470
  100.7 0.8 copy.476
  101.7 0.8 copy.474
  102.8 0.8 copy.472
  103.6 642.6 %all-gather.2.cloned.1.call-done = bf16[4096,512]{1,0:T(8,128)(2,1)} async-done(((bf16[16,512]{1,0:T(8,128)(2,1)}), bf16[4096,512]{1,0:T(8,128)(2,1)}) %all-gather.2.cloned.1.call-update) | async-done | bytes 4194320 | tf_op jit(solution)/shard_map/all_gather | solution.py:87
  746.2 2.9 convolution_convert_fusion.9
  749.2 1.0 gather_fusion.3
  750.4 1.0 copy_select_fusion.2
  751.4 32.9 %all-to-all-start = ((bf16[6,32,4,128]{3,2,0,1:T(4,128)(2,1)}), bf16[6,32,4,128]{3,2,0,1:T(4,128)(2,1)S(1)}, u32[]{:S(2)}, u32[]{:S(2)}) async-start(bf16[6,32,4,128]{3,2,0,1:T(4,128)(2,1)} %get-tuple-element.58), calls=%async_computation | async-start | bytes 393216 | tf_op jit(solution)/shard_map/all_to_all | solution.py:126
  784.3 2.3 fusion.105
  787.2 0.8 copy.477
  788.3 0.9 copy.475
  789.3 0.8 copy.473
  790.2 6.1 all-to-all-done
  796.7 1.8 fusion.115
  798.7 1.2 copy-done.10
  800.4 1.8 fusion.112
  802.9 0.9 copy-done.8
  804.2 1.8 fusion.109
  806.3 1.2 copy-done.6
  807.9 1.8 fusion.118
  810.0 1.0 copy-done.4
  811.5 1.1 pad_maximum_fusion.2
  812.6 3.9 all-to-all-start.5
  816.6 11.8 all-to-all-done.5
  828.5 0.8 gather_fusion.6
  829.3 4.6 convolution_bitcast_fusion
  833.9 9.1 copy.468
  843.0 1.0 copy-done.30
  844.2 4.1 all-to-all-start.2
  848.4 1.0 bitcast_convert_fusion.3
  849.4 10.9 all-to-all-done.2
  861.4 0.8 fusion.29
  862.7 0.9 copy-done.32
  864.1 1.0 copy.397
  865.2 1.9 stack_reshape.37
  867.1 1.7 fusion.42
  869.0 0.8 fusion.34
  870.2 0.9 copy-done.33
  872.1 1.7 fusion.43
  873.9 0.8 fusion.39
  874.7 1.2 fusion.11
  877.3 1.6 fusion.44
  879.1 0.8 fusion.24
  881.3 1.1 pad_maximum_fusion.1
  882.5 4.3 all-to-all-start.4
  887.9 1.2 copy.416
  889.1 2.4 reshape.288
  891.5 7.7 all-to-all-done.4
  899.3 1.0 gather_fusion.5
  901.1 4.7 fusion.4
  905.8 1229.2 %reduce-scatter.4.cloned.1.call-done = f32[16,512]{1,0:T(8,128)} async-done(((f32[4096,512]{1,0:T(8,128)}), f32[16,512]{1,0:T(8,128)}) %reduce-scatter.4.cloned.1.call-update) | async-done | bytes 32784 | tf_op jit(solution)/shard_map/reduce_scatter | solution.py:143
  2134.9 1.4 multiply_add_fusion
  (215 shorter events, 19.5 us)
Async XLA Ops:
  7.2 739.1 %copy-start = (bf16[1,128,1,4096]{3,1,2,0:T(8,128)(2,1)S(1)}, bf16[1,128,1,4096]{3,1,2,0:T(8,128)(2,1)}, u32[]{:S(2)}) copy-start(bf16[1,128,1,4096]{3,1,2,0:T(8,128)(2,1)} %param.15) | copy-start | bytes 3145732
  7.2 739.1 %all-gather.2.cloned.1.call-start = ((), (), s32[]{:S(2)}) async-start(), calls=%async_computation.7 | async-start | bytes 4210688 | tf_op jit(solution)/shard_map/all_gather | solution.py:87
  10.7 5.7 copy-start.2
  83.9 7.5 copy-start.3
  83.9 667.5 %all-to-all-start.3 = ((bf16[6,32,4,1024]{3,2,0,1:T(4,128)(2,1)}), bf16[6,32,4,1024]{3,2,0,1:T(4,128)(2,1)S(1)}, u32[]{:S(2)}, u32[]{:S(2)}) async-start(bf16[6,32,4,1024]{3,2,0,1:T(4,128)(2,1)} %get-tuple-element.55), calls=%async_computation.3 | async-start | bytes 3145728 | tf_op jit(solution)/shard_map/all_to_all | solution.py:125
  751.4 44.9 %all-to-all-start = ((bf16[6,32,4,128]{3,2,0,1:T(4,128)(2,1)}), bf16[6,32,4,128]{3,2,0,1:T(4,128)(2,1)S(1)}, u32[]{:S(2)}, u32[]{:S(2)}) async-start(bf16[6,32,4,128]{3,2,0,1:T(4,128)(2,1)} %get-tuple-element.58), calls=%async_computation | async-start | bytes 393216 | tf_op jit(solution)/shard_map/all_to_all | solution.py:126
  787.0 23.0 %copy-start.21 = (bf16[24,8,8,128]{3,2,1,0:T(8,128)(2,1)}, bf16[24,8,8,128]{3,2,1,0:T(8,128)(2,1)S(1)}, u32[]{:S(2)}) copy-start(bf16[24,8,8,128]{3,2,1,0:T(8,128)(2,1)S(1)} %copy.471) | copy-start | bytes 1179652
  789.1 7.6 copy-start.48
  796.6 11.3 copy-start.37
  796.6 7.6 copy-start.39
  796.6 3.8 copy-start.41
  796.7 1.8 copy-start.43
  798.5 1.8 copy-start.18
  798.5 1.4 copy-start.29
  798.5 1.8 copy-start.51
  798.7 1.2 copy-start.10
  802.2 1.9 copy-start.16
  802.2 1.5 copy-start.26
  802.9 0.9 copy-start.8
  806.0 1.8 copy-start.14
  806.1 1.4 copy-start.23
  806.2 1.2 copy-start.6
  809.7 1.6 copy-start.12
  809.9 1.1 copy-start.4
  809.9 6.6 copy-start.59
  809.9 6.6 copy-start.61
  812.6 15.8 all-to-all-start.5
  816.5 1318.5 %reduce-scatter.4.cloned.1.call-start = ((), (), s32[]{:S(2)}) async-start(), calls=%async_computation.8 | async-start | bytes 8421376 | tf_op jit(solution)/shard_map/reduce_scatter | solution.py:143
  816.6 17.4 copy-start.55
  816.6 17.3 copy-start.57
  843.0 1.0 copy-start.30
  843.0 1.1 copy-start.27
  844.0 4.3 copy-start.24
  844.2 16.1 all-to-all-start.2
  849.4 12.8 copy-start.52
  860.3 1.1 copy-start.11
  860.3 1.9 copy-start.19
  860.3 1.9 copy-start.31
  861.2 12.7 copy-start.46
  862.3 1.4 copy-start.44
  862.7 0.9 copy-start.32
  864.1 4.8 copy-start.9
  867.1 2.6 copy-start.17
  867.1 2.6 copy-start.28
  867.1 2.6 copy-start.50
  869.8 1.4 copy-start.42
  871.6 2.3 copy-start.7
  872.1 2.6 copy-start.15
  872.1 2.6 copy-start.25
  874.7 1.3 copy-start.40
  876.0 1.3 copy-start.36
  876.9 2.2 copy-start.5
  876.9 2.2 copy-start.45
  877.3 2.5 copy-start.13
  877.3 2.5 copy-start.22
  879.9 1.0 copy-start.35
  880.9 5.9 copy-start.38
  882.5 5.2 copy-start.20
  882.5 16.8 all-to-all-start.4
  891.5 8.8 copy-start.56
  900.3 1236.0 %copy-start.1 = (bf16[1,128,1,4096]{3,1,2,0:T(8,128)(2,1)S(1)}, bf16[1,128,1,4096]{3,1,2,0:T(8,128)(2,1)}, u32[]{:S(2)}) copy-start(bf16[1,128,1,4096]{3,1,2,0:T(8,128)(2,1)} %param.15) | copy-start | bytes 3145732
  901.1 1233.8 %copy-start.47 = (bf16[16,512]{1,0:T(8,128)(2,1)S(1)}, bf16[16,512]{1,0:T(8,128)(2,1)}, u32[]{:S(2)}) copy-start(bf16[16,512]{1,0:T(8,128)(2,1)} %param.19) | copy-start | bytes 49156
  901.1 1233.8 %copy-start.53 = (f32[16,512]{1,0:T(8,128)S(1)}, f32[16,512]{1,0:T(8,128)}, u32[]{:S(2)}) copy-start(f32[16,512]{1,0:T(8,128)} %param.21) | copy-start | bytes 98308
  901.1 1233.8 %copy-start.54 = (f32[16,512]{1,0:T(8,128)S(1)}, f32[16,512]{1,0:T(8,128)}, u32[]{:S(2)}) copy-start(f32[16,512]{1,0:T(8,128)} %param.20) | copy-start | bytes 98308
  (5 other events, 3.6 us)
Sparse Core Ops, SparseCore 0:
  9.9 736.3 all-gather.1
  843.1 1291.7 reduce-scatter.3
where the time goes:
time: 2150 us; the launch traced here: 2140 us
  waiting for transfers between devices  1910 us (89%)
  local copies, waits for them, and re-layouts  65.1 us (3%)
  starting transfers between devices  50.9 us (2%)
  blocking collectives  50.5 us (2%)
  matrix products  33.8 us (2%)
    reduce_scatter x1, waiting for transfers between devices, body(): lax.psum_scatter(partial_sum, ('seq', 'fsdp'), scatter_dimension=0, tiled...  1230 us
    all_gather x1, waiting for transfers between devices, fetch_weight(): return lax.all_gather(value_weight, ('seq', 'fsdp'), axis=0, tiled=True)  643 us
    all_to_all x1, blocking collectives, body(): lax.all_to_all(query_send, 'seq', split_axis=1, concat_axis=1, tiled=True)  50.5 us
  transfers between devices with their start and end apart: 7, of which 6 were waited for; matrix products, arithmetic and copies ran while one was open for 4% of the time, Pallas kernels for 0%

commit v1 on v0

v1 whole, which is shorter than its diff:
```python
import math

import jax
import jax.numpy as jnp
from jax import lax
from jax.experimental import pallas as pl
from jax.experimental.pallas import tpu as pltpu
from jax.sharding import PartitionSpec as P


KVH = 4
HD = 128
GROUP = 8
LANES = 32
PEERS = 8
CAP = 6
CAP8 = 8
ROUNDS = 128
WROWS = 16
HROWS = CAP * GROUP
MROWS = HROWS + WROWS + CAP8
ROWS = LANES * HROWS
KEYS = LANES * CAP8
CHUNKS = 6
CHUNK = ROWS // CHUNKS
SCORE_NEG = -1e30
EWC_LAMBDA = 4.0
SCALE = 1.0 / math.sqrt(HD)
BF = jnp.bfloat16
F32 = jnp.float32


def exchange(value, axes):
    return lax.all_to_all(value, axes, split_axis=0, concat_axis=0, tiled=True)


def round_plan(starts, owner_list):
    round_ids = jnp.arange(ROUNDS, dtype=jnp.int32)
    start_rounds = starts // LANES
    doc_of = jnp.sum((start_rounds[None, :] <= round_ids[:, None]).astype(jnp.int32), axis=1) - 1
    doc_ids = jnp.arange(starts.shape[0], dtype=jnp.int32)
    onehot = (doc_of[:, None] == doc_ids[None, :]).astype(jnp.int32)
    owner_of = jnp.sum(onehot * owner_list[None, :], axis=1)
    earlier = (owner_of[:, None] == owner_of[None, :]) & (round_ids[None, :] < round_ids[:, None])
    rank_of = jnp.sum(earlier.astype(jnp.int32), axis=1)
    return doc_of, owner_of, rank_of


def pick_rows(code, count):
    slots = lax.broadcasted_iota(jnp.int32, (count, ROUNDS), 0)
    return (slots == code).astype(F32).astype(BF)


def spread_heads(code, x_ref, acc_ref):
    rows = jnp.dot(pick_rows(code, CAP * LANES), x_ref[...], preferred_element_type=F32)
    for g in range(GROUP):
        for s in range(CAP):
            acc_ref[pl.ds(s * GROUP + g, LANES, stride=HROWS), :] = rows[
                s * LANES : (s + 1) * LANES, g * HD : (g + 1) * HD
            ]
    return acc_ref[...].astype(BF).reshape(LANES, HROWS, HD)


def pack_grad_kernel(code_ref, g_ref, out_ref, acc_ref):
    out_ref[:, 0] = spread_heads(code_ref[0:1, :], g_ref, acc_ref)


def pack_query_kernel(code_ref, q_ref, k_ref, w_ref, out_ref, acc_ref):
    out_ref[:, 0, 0:HROWS] = spread_heads(code_ref[0:1, :], q_ref, acc_ref)
    out_ref[:, 0, HROWS : HROWS + WROWS] = jnp.broadcast_to(w_ref[...][None], (LANES, WROWS, HD))
    keys = jnp.dot(pick_rows(code_ref[1:2, :], KEYS), k_ref[...], preferred_element_type=F32)
    out_ref[:, 0, HROWS + WROWS :] = keys.reshape(LANES, CAP8, HD).astype(BF)


def code_spec():
    return pl.BlockSpec((2, ROUNDS), lambda h: (0, 0))


def head_spec(rows):
    return pl.BlockSpec((LANES, 1, rows, HD), lambda h: (0, h, 0, 0))


def key_spec():
    return pl.BlockSpec((LANES, CAP8, HD), lambda h: (0, 0, h))


def probs_spec():
    return pl.BlockSpec((1, ROWS, KEYS), lambda h: (h, 0, 0))


def pack_query(codes, queries, keys, weight):
    return pl.pallas_call(
        pack_query_kernel,
        grid=(KVH,),
        in_specs=[
            code_spec(),
            pl.BlockSpec((ROUNDS, GROUP * HD), lambda h: (0, h)),
            pl.BlockSpec((ROUNDS, HD), lambda h: (0, h)),
            pl.BlockSpec((WROWS, HD), lambda h: (0, h)),
        ],
        out_specs=head_spec(MROWS),
        out_shape=jax.ShapeDtypeStruct((LANES, KVH, MROWS, HD), BF),
        scratch_shapes=[pltpu.VMEM((ROWS, HD), F32)],
        name="pack_query",
    )(codes, queries, keys, weight)


def pack_grad(codes, grads):
    return pl.pallas_call(
        pack_grad_kernel,
        grid=(KVH,),
        in_specs=[code_spec(), pl.BlockSpec((ROUNDS, GROUP * HD), lambda h: (0, h))],
        out_specs=head_spec(HROWS),
        out_shape=jax.ShapeDtypeStruct((LANES, KVH, HROWS, HD), BF),
        scratch_shapes=[pltpu.VMEM((ROWS, HD), F32)],
        name="pack_grad",
    )(codes, grads)


def mix_matrix(turned):
    a = lax.broadcasted_iota(jnp.int32, (1024, 1024), 1 if turned else 0)
    b = lax.broadcasted_iota(jnp.int32, (1024, 1024), 0 if turned else 1)
    target = ((a >> 4) & 7) * 128 + (a >> 7) * 16 + (a & 15)
    return (target == b).astype(F32).astype(BF)


def split_kernel(x_ref, out_ref, mix_ref):
    @pl.when(pl.program_id(0) == 0)
    def _():
        mix_ref[...] = mix_matrix(False)

    mixed = jnp.dot(x_ref[...], mix_ref[...], preferred_element_type=F32)
    for f in range(PEERS):
        out_ref[f] = mixed[:, f * 128 : (f + 1) * 128].astype(BF)


def split_features(rows):
    return pl.pallas_call(
        split_kernel,
        grid=(4,),
        in_specs=[pl.BlockSpec((ROUNDS, 1024), lambda q: (0, q))],
        out_specs=pl.BlockSpec((PEERS, ROUNDS, 128), lambda q: (0, 0, q)),
        out_shape=jax.ShapeDtypeStruct((PEERS, ROUNDS, 512), BF),
        scratch_shapes=[pltpu.VMEM((1024, 1024), BF)],
        name="split_features",
    )(rows)


def join_kernel(x_ref, out_ref, mix_ref):
    @pl.when(pl.program_id(0) == 0)
    def _():
        mix_ref[...] = mix_matrix(True)

    parts = jnp.concatenate([x_ref[f] for f in range(PEERS)], axis=1)
    out_ref[...] = jnp.dot(parts, mix_ref[...], preferred_element_type=F32).astype(BF)


def join_features(parts):
    return pl.pallas_call(
        join_kernel,
        grid=(4,),
        in_specs=[pl.BlockSpec((PEERS, ROUNDS, 128), lambda q: (0, 0, q))],
        out_specs=pl.BlockSpec((ROUNDS, 1024), lambda q: (0, q)),
        out_shape=jax.ShapeDtypeStruct((ROUNDS, 4096), BF),
        scratch_shapes=[pltpu.VMEM((1024, 1024), BF)],
        name="join_features",
    )(parts)


def doc_table(slot, doc_ref):
    table = jnp.full(slot.shape, -2, jnp.int32)
    for s in range(CAP):
        table = jnp.where(slot == s, doc_ref[s], table)
    return table


def own_keys(block_ref):
    return block_ref[:, 0, HROWS + WROWS :].astype(F32).reshape(KEYS, HD).astype(BF)


def probs_kernel(doc_ref, own_ref, p_ref, bias_ref):
    @pl.when(pl.program_id(0) == 0)
    def _():
        shape = (LANES, HROWS, KEYS)
        q_lane = lax.broadcasted_iota(jnp.int32, shape, 0)
        q_slot = lax.broadcasted_iota(jnp.int32, shape, 1) >> 3
        key = lax.broadcasted_iota(jnp.int32, shape, 2)
        k_lane = key >> 3
        k_slot = key & 7
        seen = (doc_table(q_slot, doc_ref) == doc_table(k_slot, doc_ref)) & (
            k_slot * LANES + k_lane <= q_slot * LANES + q_lane
        )
        bias_ref[...] = jnp.where(seen, 0.0, SCORE_NEG).astype(F32).reshape(ROWS, KEYS)

    query = own_ref[:, 0, 0:HROWS].reshape(ROWS, HD)
    keys = own_keys(own_ref)
    for c in range(CHUNKS):
        rows = slice(c * CHUNK, (c + 1) * CHUNK)
        scores = lax.dot_general(
            query[rows], keys, (((1,), (1,)), ((), ())), preferred_element_type=F32
        )
        scores = scores * SCALE + bias_ref[rows, :]
        peak = jnp.max(scores, axis=1, keepdims=True)
        weight = jnp.exp(scores - peak)
        total = jnp.sum(weight, axis=1, keepdims=True)
        p_ref[0, rows, :] = (weight * (1.0 / total)).astype(BF)


def attend_probs(slot_doc, own):
    return pl.pallas_call(
        probs_kernel,
        grid=(KVH,),
        in_specs=[pl.BlockSpec(memory_space=pltpu.SMEM), head_spec(MROWS)],
        out_specs=probs_spec(),
        out_shape=jax.ShapeDtypeStruct((KVH, ROWS, KEYS), BF),
        scratch_shapes=[pltpu.VMEM((ROWS, KEYS), F32)],
        name="attend_probs",
    )(slot_doc, own)


def value_kernel(p_ref, g_ref, dv_ref):
    grad = g_ref[...].reshape(ROWS, HD)
    turned = lax.dot_general(
        grad, p_ref[0], (((0,), (0,)), ((), ())), preferred_element_type=F32
    )
    dv_ref[...] = turned.T.astype(BF).reshape(LANES, CAP8, HD)


def attend_value(probs, grad):
    return pl.pallas_call(
        value_kernel,
        grid=(KVH,),
        in_specs=[probs_spec(), head_spec(HROWS)],
        out_specs=key_spec(),
        out_shape=jax.ShapeDtypeStruct((LANES, CAP8, KVH * HD), BF),
        name="attend_value",
    )(probs, grad)


def query_kernel(p_ref, own_ref, g_ref, v_ref, dq_ref, dk_ref, ds_ref, acc_ref):
    query = own_ref[:, 0, 0:HROWS].reshape(ROWS, HD)
    keys = own_keys(own_ref)
    grad = g_ref[...].reshape(ROWS, HD)
    values = v_ref[...].astype(F32).reshape(KEYS, HD).astype(BF)
    for c in range(CHUNKS):
        rows = slice(c * CHUNK, (c + 1) * CHUNK)
        probs = p_ref[0, rows, :]
        grad_c = grad[rows]
        attn = jnp.dot(probs, values, preferred_element_type=F32).astype(BF)
        delta = jnp.sum(grad_c.astype(F32) * attn.astype(F32), axis=1, keepdims=True)
        dprobs = lax.dot_general(
            grad_c, values, (((1,), (1,)), ((), ())), preferred_element_type=F32
        )
        dscores = (probs.astype(F32) * (dprobs - delta) * SCALE).astype(BF)
        ds_ref[rows, :] = dscores
        acc_ref[rows, :] = jnp.dot(dscores, keys, preferred_element_type=F32)
    for g in range(GROUP):
        for s in range(CAP):
            dq_ref[s, :, g * HD : (g + 1) * HD] = acc_ref[
                pl.ds(s * GROUP + g, LANES, stride=HROWS), :
            ].astype(BF)
    turned = lax.dot_general(
        query, ds_ref[...], (((0,), (0,)), ((), ())), preferred_element_type=F32
    )
    dk_ref[...] = turned.T.astype(BF).reshape(LANES, CAP8, HD)


def attend_query(probs, own, grad, values):
    return pl.pallas_call(
        query_kernel,
        grid=(KVH,),
        in_specs=[probs_spec(), head_spec(MROWS), head_spec(HROWS), key_spec()],
        out_specs=(pl.BlockSpec((CAP, LANES, GROUP * HD), lambda h: (0, 0, h)), key_spec()),
        out_shape=(
            jax.ShapeDtypeStruct((CAP, LANES, KVH * GROUP * HD), BF),
            jax.ShapeDtypeStruct((LANES, CAP8, KVH * HD), BF),
        ),
        scratch_shapes=[pltpu.VMEM((ROWS, KEYS), BF), pltpu.VMEM((ROWS, HD), F32)],
        name="attend_query",
    )(probs, own, grad, values)


def body(inputs, queries, rotated_keys, out_grad, value_weight, fisher, anchor, doc_starts, owners):
    own_lane = lax.axis_index("seq")
    token_rows = inputs.reshape(ROUNDS, -1)
    query_rows = queries.reshape(ROUNDS, -1)
    key_rows = rotated_keys.reshape(ROUNDS, -1)
    grad_rows = out_grad.reshape(ROUNDS, -1)
    doc_of, owner_of, rank_of = round_plan(doc_starts[0], owners[0])
    home_code = owner_of * CAP8 + rank_of
    codes = jnp.stack([rank_of * LANES + owner_of, home_code])
    slot_ids = jnp.arange(CAP8, dtype=jnp.int32)
    mine = (owner_of[None, :] == own_lane) & (rank_of[None, :] == slot_ids[:, None])
    slot_doc = jnp.sum(jnp.where(mine, doc_of[None, :] + 1, 0), axis=1) - 1
    pick = (jnp.arange(KEYS, dtype=jnp.int32)[:, None] == home_code[None, :]).astype(BF)

    def place(rows):
        return jnp.dot(pick, rows, preferred_element_type=F32).astype(BF).reshape(LANES, CAP8, -1)

    def collect(slots):
        return lax.dot_general(
            pick, slots.reshape(KEYS, -1), (((0,), (0,)), ((), ())), preferred_element_type=F32
        ).astype(BF)

    own = exchange(pack_query(codes, query_rows, key_rows, value_weight), "seq")
    token_split = split_features(token_rows)
    grad_split = pack_grad(codes, grad_rows)
    token_split, own = lax.optimization_barrier((token_split, own))
    token_part = exchange(token_split, "fsdp").reshape(PEERS * ROUNDS, -1)
    probs = attend_probs(slot_doc, own)
    weight_part = own[:, :, HROWS : HROWS + WROWS].transpose(0, 2, 1, 3).reshape(LANES * WROWS, -1)
    grad_split, token_part = lax.optimization_barrier((grad_split, token_part))
    grad_own = exchange(grad_split, "seq")
    value_part = jnp.dot(token_part, weight_part, preferred_element_type=F32).astype(BF)
    value_part, grad_own = lax.optimization_barrier((value_part, grad_own))
    value_parts = exchange(value_part.reshape(PEERS, ROUNDS, -1), "fsdp")
    value_back = attend_value(probs, grad_own)
    values = jnp.sum(value_parts.astype(F32), axis=0).astype(BF)

    both = exchange(jnp.concatenate([place(values), value_back], axis=1), "seq")
    value_home = collect(both[:, CAP8:])
    value_all = exchange(
        jnp.broadcast_to(value_home[None], (PEERS,) + value_home.shape), "fsdp"
    ).reshape(PEERS * ROUNDS, -1)
    query_out, key_back = attend_query(probs, own, grad_own, both)

    input_part = lax.dot_general(
        value_all, weight_part, (((1,), (1,)), ((), ())), preferred_element_type=F32
    ).astype(BF)
    input_parts = exchange(input_part.reshape(PEERS, ROUNDS, -1), "fsdp")
    weight_grad = lax.dot_general(
        token_part, value_all, (((0,), (0,)), ((), ())), preferred_element_type=F32
    ).astype(BF)
    back = jnp.concatenate([weight_grad.reshape(LANES, WROWS, -1), key_back], axis=1)
    back, input_parts = lax.optimization_barrier((back, input_parts))
    last = exchange(back, "seq")
    input_grad = join_features(input_parts)
    weight_sum = jnp.sum(last[:, :WROWS].astype(F32), axis=0)
    key_home = collect(last[:, WROWS:])

    tokens_total = ROUNDS * LANES * PEERS
    ewc_grad = weight_sum * (1.0 / math.sqrt(tokens_total)) + EWC_LAMBDA * fisher * (
        value_weight.astype(F32) - anchor
    )
    return (
        query_out.reshape(1, 1, CAP, LANES, -1),
        key_home.reshape(1, ROUNDS, 1, -1),
        input_grad.reshape(1, ROUNDS, 1, -1),
        ewc_grad,
    )


def solution(mesh):
    rows = P("fsdp", None, "seq", None)
    weights = P(("seq", "fsdp"), None)
    plan = P("fsdp", None)
    return jax.shard_map(
        body,
        mesh=mesh,
        in_specs=(rows, rows, rows, rows, weights, weights, weights, plan, plan),
        out_specs=(P("fsdp", "seq", None, None, None), rows, rows, weights),
        check_vma=False,
    )
```

time: 2150 us -> 254 us (0.12)
  the two profiles are of different devices: /device:TPU:0 before, /device:TPU:33 now
where the time goes in v1:
time: 254 us; the launch traced here: 253 us
  waiting for transfers between devices  128 us (50%)
  blocking collectives  39.9 us (16%)
  Pallas kernels  37.3 us (15%)
  starting transfers between devices  34.6 us (14%)
  other arithmetic  5.75 us (2%)
  matrix products  5.44 us (2%)
    all_to_all x6, waiting for transfers between devices, exchange(): return lax.all_to_all(value, axes, split_axis=0, concat_axis=0, tiled=True)  128 us
    all_to_all x2, blocking collectives, exchange(): return lax.all_to_all(value, axes, split_axis=0, concat_axis=0, tiled=True)  39.9 us
    all_to_all x6, starting transfers between devices, exchange(): return lax.all_to_all(value, axes, split_axis=0, concat_axis=0, tiled=True)  34.6 us
    pallas_call x1, Pallas kernels, attend_query(): pl.pallas_call(query_kernel, grid=(KVH,), in_specs=[probs_spec(), head_sp...  8.88 us
    pallas_call x1, Pallas kernels, attend_probs(): pl.pallas_call(probs_kernel, grid=(KVH,), in_specs=[pl.BlockSpec(memory_s...  5.7 us
  transfers between devices with their start and end apart: 6, of which 6 were waited for; matrix products, arithmetic and copies ran while one was open for 2% of the time, Pallas kernels for 13%

profile of v1, /device:TPU:33, one launch (start us, length us, event | category | flops | bytes accessed | tf_op | source)
XLA Modules:
  0.0 253.2 jit_solution(2695236318013879010)
XLA Ops:
  0.6 0.7 fusion.12
  1.3 0.1 convert_reduce_fusion.2
  1.4 0.7 select_reduce_fusion
  2.1 0.2 convert_reduce_fusion.1
  2.3 0.6 pad_add_fusion.code_ref
  2.9 4.6 %pack_query.1 = bf16[32,4,72,128]{3,2,1,0:T(8,128)(2,1)} custom-call(s32[2,128]{1,0:T(2,128)} %pad_add_fusion.code_ref, bf16[128,4096]{1,0:T(8,128)(2,1)} %bitcast.55, bf16[128,512]{1,0:T(8,128)(2,1)} %bitcast.59, bf16[16,512]{1,0:T(8,128)(2,1)} %w_ref.1), custom_call_target="tpu_custom_call" | custom-call | tf_op jit(solution)/shard_map/pack_query/pallas_call | solution.py:92
  7.5 10.9 %all-to-all-start = ((bf16[32,4,72,128]{3,2,1,0:T(8,128)(2,1)}), bf16[32,4,72,128]{3,2,1,0:T(8,128)(2,1)S(1)}, u32[]{:S(2)}, u32[]{:S(2)}) async-start(bf16[32,4,72,128]{3,2,1,0:T(8,128)(2,1)} %pack_query.1), calls=%async_computation | async-start | bytes 4718592 | tf_op jit(solution)/shard_map/all_to_all | solution.py:34
  18.3 4.7 %split_features.1 = bf16[8,128,512]{2,1,0:T(8,128)(2,1)} custom-call(bf16[128,4096]{1,0:T(8,128)(2,1)} %bitcast.49), custom_call_target="tpu_custom_call" | custom-call | tf_op jit(solution)/shard_map/split_features/pallas_call | solution.py:138
  23.1 52.8 %all-to-all-done.own_ref = bf16[32,4,72,128]{3,2,1,0:T(8,128)(2,1)S(1)} async-done(((bf16[32,4,72,128]{3,2,1,0:T(8,128)(2,1)}), bf16[32,4,72,128]{3,2,1,0:T(8,128)(2,1)S(1)}, u32[]{:S(2)}, u32[]{:S(2)}) %all-to-all-start) | async-done | bytes 2359328 | tf_op jit(solution)/shard_map/all_to_all | solution.py:34
  75.9 0.0 copy-start
  75.9 5.4 %all-to-all-start.1 = ((bf16[8,128,512]{2,1,0:T(8,128)(2,1)}), bf16[8,128,512]{2,1,0:T(8,128)(2,1)S(1)}, u32[]{:S(2)}, u32[]{:S(2)}) async-start(bf16[8,128,512]{2,1,0:T(8,128)(2,1)} %split_features.1), calls=%async_computation.1 | async-start | bytes 2097152 | tf_op jit(solution)/shard_map/all_to_all | solution.py:34
  81.3 4.2 %pack_grad.1 = bf16[32,4,48,128]{3,2,1,0:T(8,128)(2,1)} custom-call(s32[2,128]{1,0:T(2,128)} %pad_add_fusion.code_ref, bf16[128,4096]{1,0:T(8,128)(2,1)} %bitcast.48), custom_call_target="tpu_custom_call" | custom-call | tf_op jit(solution)/shard_map/pack_grad/pallas_call | solution.py:109
  85.4 10.5 %all-to-all-done.1 = bf16[8,128,512]{2,1,0:T(8,128)(2,1)S(1)} async-done(((bf16[8,128,512]{2,1,0:T(8,128)(2,1)}), bf16[8,128,512]{2,1,0:T(8,128)(2,1)S(1)}, u32[]{:S(2)}, u32[]{:S(2)}) %all-to-all-start.1) | async-done | bytes 1048608 | tf_op jit(solution)/shard_map/all_to_all | solution.py:34
  95.9 5.1 %all-to-all-start.2 = ((bf16[32,4,48,128]{3,2,1,0:T(8,128)(2,1)}), bf16[32,4,48,128]{3,2,1,0:T(8,128)(2,1)}, u32[]{:S(2)}, u32[]{:S(2)}) async-start(bf16[32,4,48,128]{3,2,1,0:T(8,128)(2,1)} %pack_grad.1), calls=%async_computation.2 | async-start | bytes 3145728 | tf_op jit(solution)/shard_map/all_to_all | solution.py:34
  101.0 0.0 copy-done
  101.1 0.1 slice_bitcast_fusion
  101.1 0.3 copy.14
  101.4 0.0 copy-start.3
  101.4 0.8 copy-done.3
  102.2 1.7 convolution_convert_fusion.1
  103.9 37.9 %all-to-all-done.2.g_ref = bf16[32,4,48,128]{3,2,1,0:T(8,128)(2,1)} async-done(((bf16[32,4,48,128]{3,2,1,0:T(8,128)(2,1)}), bf16[32,4,48,128]{3,2,1,0:T(8,128)(2,1)}, u32[]{:S(2)}, u32[]{:S(2)}) %all-to-all-start.2) | async-done | bytes 1572896 | tf_op jit(solution)/shard_map/all_to_all | solution.py:34
  141.8 3.7 %all-to-all-start.3 = ((bf16[8,128,512]{2,1,0:T(8,128)(2,1)}), bf16[8,128,512]{2,1,0:T(8,128)(2,1)S(1)}, u32[]{:S(2)}, u32[]{:S(2)}) async-start(bf16[8,128,512]{2,1,0:T(8,128)(2,1)} %bitcast.10), calls=%async_computation.3 | async-start | bytes 2097152 | tf_op jit(solution)/shard_map/all_to_all | solution.py:34
  145.5 0.1 select_reduce_fusion.1
  145.6 0.5 broadcast_add_fusion.doc_ref
  146.2 5.7 %attend_probs.1.p_ref = bf16[4,1536,256]{2,1,0:T(8,128)(2,1)} custom-call(s32[8]{0:T(128)} %broadcast_add_fusion.doc_ref, bf16[32,4,72,128]{3,2,1,0:T(8,128)(2,1)} %copy-done), custom_call_target="tpu_custom_call" | custom-call | tf_op jit(solution)/shard_map/attend_probs/pallas_call | solution.py:210
  151.9 4.6 %attend_value.1 = bf16[32,8,512]{2,1,0:T(8,128)(2,1)} custom-call(bf16[4,1536,256]{2,1,0:T(8,128)(2,1)} %attend_probs.1.p_ref, bf16[32,4,48,128]{3,2,1,0:T(8,128)(2,1)} %all-to-all-done.2.g_ref), custom_call_target="tpu_custom_call" | custom-call | tf_op jit(solution)/shard_map/attend_value/pallas_call | solution.py:230
  156.4 3.7 %all-to-all-done.3 = bf16[8,128,512]{2,1,0:T(8,128)(2,1)S(1)} async-done(((bf16[8,128,512]{2,1,0:T(8,128)(2,1)}), bf16[8,128,512]{2,1,0:T(8,128)(2,1)S(1)}, u32[]{:S(2)}, u32[]{:S(2)}) %all-to-all-start.3) | async-done | bytes 1048608 | tf_op jit(solution)/shard_map/all_to_all | solution.py:34
  160.2 0.1 reduce_sum.67
  160.3 0.2 fusion
  160.6 1.0 pad_maximum_fusion.1
  161.6 22.6 %all_to_all.40.v_ref = bf16[32,16,512]{2,1,0:T(8,128)(2,1)S(1)} all-to-all(bf16[32,16,512]{2,1,0:T(8,128)(2,1)S(1)} %pad_maximum_fusion.1), channel_id=1, replica_groups=mesh['seq'=32,'fsdp'=8] {'seq'}, dimensions={0} | all-to-all | bytes 1048576 | tf_op jit(solution)/shard_map/all_to_all | solution.py:34
  184.1 0.0 copy-start.2
  184.1 0.0 copy-start.4
  184.1 0.2 convolution_convert_fusion.5
  184.4 0.1 broadcast_in_dim.12
  184.5 17.3 %all_to_all.41 = bf16[8,128,512]{2,1,0:T(8,128)(2,1)S(1)} all-to-all(bf16[8,128,512]{2,1,0:T(8,128)(2,1)S(1)} %broadcast_in_dim.12), channel_id=1, replica_groups=mesh['seq'=32,'fsdp'=8] {'fsdp'}, dimensions={0} | all-to-all | bytes 2097152 | tf_op jit(solution)/shard_map/all_to_all | solution.py:34
  201.8 0.0 copy-done.4
  201.8 1.7 convolution_convert_fusion
  203.5 0.0 copy-done.2
  203.5 4.8 %all-to-all-start.6 = ((bf16[8,128,512]{2,1,0:T(8,128)(2,1)}), bf16[8,128,512]{2,1,0:T(8,128)(2,1)S(1)}, u32[]{:S(2)}, u32[]{:S(2)}) async-start(bf16[8,128,512]{2,1,0:T(8,128)(2,1)} %bitcast.16), calls=%async_computation.6 | async-start | bytes 2097152 | tf_op jit(solution)/shard_map/all_to_all | solution.py:34
  208.3 8.9 %attend_query.1 = (bf16[6,32,4096]{2,1,0:T(8,128)(2,1)}, bf16[32,8,512]{2,1,0:T(8,128)(2,1)}) custom-call(bf16[4,1536,256]{2,1,0:T(8,128)(2,1)} %attend_probs.1.p_ref, bf16[32,4,72,128]{3,2,1,0:T(8,128)(2,1)} %copy-done, bf16[32,4,48,128]{3,2,1,0:T(8,128)(2,1)} %all-to-all-done.2.g_ref, bf16[32,16,512]{2,1,0:T(8,128)(2,1)} %copy-done.2), custom_call_target="tpu_custom_call" | custom-call | tf_op jit(solution)/shard_map/attend_query/pallas_call | solution.py:269
  217.1 0.0 copy-start.5
  217.1 0.7 convolution_convert_fusion.2
  217.9 0.2 copy-done.5
  218.1 1.0 pad_maximum_fusion
  219.1 0.0 copy-start.6
  219.1 0.0 copy-start.7
  219.1 0.0 copy-start.8
  219.1 3.9 %all-to-all-done.6.x_ref = bf16[8,128,512]{2,1,0:T(8,128)(2,1)S(1)} async-done(((bf16[8,128,512]{2,1,0:T(8,128)(2,1)}), bf16[8,128,512]{2,1,0:T(8,128)(2,1)S(1)}, u32[]{:S(2)}, u32[]{:S(2)}) %all-to-all-start.6) | async-done | bytes 1048608 | tf_op jit(solution)/shard_map/all_to_all | solution.py:34
  222.9 0.0 copy-start.1
  222.9 4.8 %all-to-all-start.7 = ((bf16[32,24,512]{2,1,0:T(8,128)(2,1)}), bf16[32,24,512]{2,1,0:T(8,128)(2,1)S(1)}, u32[]{:S(2)}, u32[]{:S(2)}) async-start(bf16[32,24,512]{2,1,0:T(8,128)(2,1)} %pad_maximum_fusion), calls=%async_computation.7 | async-start | bytes 1572864 | tf_op jit(solution)/shard_map/all_to_all | solution.py:34
  227.8 0.0 copy-done.1
  227.8 4.6 %join_features.1 = bf16[128,4096]{1,0:T(8,128)(2,1)} custom-call(bf16[8,128,512]{2,1,0:T(8,128)(2,1)} %copy-done.1), custom_call_target="tpu_custom_call" | custom-call | tf_op jit(solution)/shard_map/join_features/pallas_call | solution.py:159
  232.4 19.2 %all-to-all-done.7 = bf16[32,24,512]{2,1,0:T(8,128)(2,1)S(1)} async-done(((bf16[32,24,512]{2,1,0:T(8,128)(2,1)}), bf16[32,24,512]{2,1,0:T(8,128)(2,1)S(1)}, u32[]{:S(2)}, u32[]{:S(2)}) %all-to-all-start.7) | async-done | bytes 786464 | tf_op jit(solution)/shard_map/all_to_all | solution.py:34
  251.6 0.1 convert_reduce_fusion
  251.6 0.0 copy-done.6
  251.7 0.0 copy-done.7
  251.7 0.0 copy-done.8
  251.7 0.6 multiply_add_fusion
  252.3 0.9 fusion.1
  (4 shorter events, 0.0 us)
Async XLA Ops:
  7.5 68.4 %all-to-all-start = ((bf16[32,4,72,128]{3,2,1,0:T(8,128)(2,1)}), bf16[32,4,72,128]{3,2,1,0:T(8,128)(2,1)S(1)}, u32[]{:S(2)}, u32[]{:S(2)}) async-start(bf16[32,4,72,128]{3,2,1,0:T(8,128)(2,1)} %pack_query.1), calls=%async_computation | async-start | bytes 4718592 | tf_op jit(solution)/shard_map/all_to_all | solution.py:34
  75.9 25.2 %copy-start = (bf16[32,4,72,128]{3,2,1,0:T(8,128)(2,1)}, bf16[32,4,72,128]{3,2,1,0:T(8,128)(2,1)S(1)}, u32[]{:S(2)}) copy-start(bf16[32,4,72,128]{3,2,1,0:T(8,128)(2,1)S(1)} %all-to-all-done.own_ref) | copy-start | bytes 7077892
  75.9 20.1 %all-to-all-start.1 = ((bf16[8,128,512]{2,1,0:T(8,128)(2,1)}), bf16[8,128,512]{2,1,0:T(8,128)(2,1)S(1)}, u32[]{:S(2)}, u32[]{:S(2)}) async-start(bf16[8,128,512]{2,1,0:T(8,128)(2,1)} %split_features.1), calls=%async_computation.1 | async-start | bytes 2097152 | tf_op jit(solution)/shard_map/all_to_all | solution.py:34
  95.9 45.9 %all-to-all-start.2 = ((bf16[32,4,48,128]{3,2,1,0:T(8,128)(2,1)}), bf16[32,4,48,128]{3,2,1,0:T(8,128)(2,1)}, u32[]{:S(2)}, u32[]{:S(2)}) async-start(bf16[32,4,48,128]{3,2,1,0:T(8,128)(2,1)} %pack_grad.1), calls=%async_computation.2 | async-start | bytes 3145728 | tf_op jit(solution)/shard_map/all_to_all | solution.py:34
  101.4 0.8 copy-start.3
  141.8 18.4 %all-to-all-start.3 = ((bf16[8,128,512]{2,1,0:T(8,128)(2,1)}), bf16[8,128,512]{2,1,0:T(8,128)(2,1)S(1)}, u32[]{:S(2)}, u32[]{:S(2)}) async-start(bf16[8,128,512]{2,1,0:T(8,128)(2,1)} %bitcast.10), calls=%async_computation.3 | async-start | bytes 2097152 | tf_op jit(solution)/shard_map/all_to_all | solution.py:34
  184.1 19.4 %copy-start.2 = (bf16[32,16,512]{2,1,0:T(8,128)(2,1)}, bf16[32,16,512]{2,1,0:T(8,128)(2,1)S(1)}, u32[]{:S(2)}) copy-start(bf16[32,16,512]{2,1,0:T(8,128)(2,1)S(1)} %all_to_all.40.v_ref) | copy-start | bytes 1572868
  184.1 17.6 %copy-start.4 = (bf16[32,16,4,128]{3,2,1,0:T(4,128)(2,1)S(1)}, bf16[32,16,4,128]{3,2,1,0:T(4,128)(2,1)}, u32[]{:S(2)}) copy-start(bf16[32,16,4,128]{3,2,1,0:T(4,128)(2,1)} %copy-done.3) | copy-start | bytes 1572868
  203.5 19.4 %all-to-all-start.6 = ((bf16[8,128,512]{2,1,0:T(8,128)(2,1)}), bf16[8,128,512]{2,1,0:T(8,128)(2,1)S(1)}, u32[]{:S(2)}, u32[]{:S(2)}) async-start(bf16[8,128,512]{2,1,0:T(8,128)(2,1)} %bitcast.16), calls=%async_computation.6 | async-start | bytes 2097152 | tf_op jit(solution)/shard_map/all_to_all | solution.py:34
  217.1 0.9 copy-start.5
  219.1 32.6 %copy-start.6 = (bf16[16,512]{1,0:T(8,128)(2,1)S(1)}, bf16[16,512]{1,0:T(8,128)(2,1)}, u32[]{:S(2)}) copy-start(bf16[16,512]{1,0:T(8,128)(2,1)} %w_ref.1) | copy-start | bytes 49156
  219.1 32.6 %copy-start.7 = (f32[16,512]{1,0:T(8,128)S(1)}, f32[16,512]{1,0:T(8,128)}, u32[]{:S(2)}) copy-start(f32[16,512]{1,0:T(8,128)} %param.15) | copy-start | bytes 98308
  219.1 32.6 %copy-start.8 = (f32[16,512]{1,0:T(8,128)S(1)}, f32[16,512]{1,0:T(8,128)}, u32[]{:S(2)}) copy-start(f32[16,512]{1,0:T(8,128)} %param.14) | copy-start | bytes 98308
  222.9 4.8 %copy-start.1 = (bf16[8,128,512]{2,1,0:T(8,128)(2,1)}, bf16[8,128,512]{2,1,0:T(8,128)(2,1)S(1)}, u32[]{:S(2)}) copy-start(bf16[8,128,512]{2,1,0:T(8,128)(2,1)S(1)} %all-to-all-done.6.x_ref) | copy-start | bytes 3145732
  222.9 28.6 %all-to-all-start.7 = ((bf16[32,24,512]{2,1,0:T(8,128)(2,1)}), bf16[32,24,512]{2,1,0:T(8,128)(2,1)S(1)}, u32[]{:S(2)}, u32[]{:S(2)}) async-start(bf16[32,24,512]{2,1,0:T(8,128)(2,1)} %pad_maximum_fusion), calls=%async_computation.7 | async-start | bytes 1572864 | tf_op jit(solution)/shard_map/all_to_all | solution.py:34

commit v2 on v1

--- a/solution.py
+++ b/solution.py
@@ -5,7 +5,7 @@
 from jax import lax
 from jax.experimental import pallas as pl
 from jax.experimental.pallas import tpu as pltpu
-from jax.sharding import PartitionSpec as P
+from jax.sharding import Mesh, PartitionSpec as P
 
 
 KVH = 4
@@ -13,12 +13,16 @@
 GROUP = 8
 LANES = 32
 PEERS = 8
+FEATS = 512
+RING = 4
+FEAT = ("zl", "y")
+SEQ = ("zh", "x", "core")
 CAP = 6
 CAP8 = 8
 ROUNDS = 128
 WROWS = 16
 HROWS = CAP * GROUP
-MROWS = HROWS + WROWS + CAP8
+MROWS = HROWS + CAP8
 ROWS = LANES * HROWS
 KEYS = LANES * CAP8
 CHUNKS = 6
@@ -65,11 +69,10 @@
     out_ref[:, 0] = spread_heads(code_ref[0:1, :], g_ref, acc_ref)
 
 
-def pack_query_kernel(code_ref, q_ref, k_ref, w_ref, out_ref, acc_ref):
+def pack_query_kernel(code_ref, q_ref, k_ref, out_ref, acc_ref):
     out_ref[:, 0, 0:HROWS] = spread_heads(code_ref[0:1, :], q_ref, acc_ref)
-    out_ref[:, 0, HROWS : HROWS + WROWS] = jnp.broadcast_to(w_ref[...][None], (LANES, WROWS, HD))
     keys = jnp.dot(pick_rows(code_ref[1:2, :], KEYS), k_ref[...], preferred_element_type=F32)
-    out_ref[:, 0, HROWS + WROWS :] = keys.reshape(LANES, CAP8, HD).astype(BF)
+    out_ref[:, 0, HROWS:] = keys.reshape(LANES, CAP8, HD).astype(BF)
 
 
 def code_spec():
@@ -88,7 +91,7 @@
     return pl.BlockSpec((1, ROWS, KEYS), lambda h: (h, 0, 0))
 
 
-def pack_query(codes, queries, keys, weight):
+def pack_query(codes, queries, keys):
     return pl.pallas_call(
         pack_query_kernel,
         grid=(KVH,),
@@ -96,13 +99,12 @@
             code_spec(),
             pl.BlockSpec((ROUNDS, GROUP * HD), lambda h: (0, h)),
             pl.BlockSpec((ROUNDS, HD), lambda h: (0, h)),
-            pl.BlockSpec((WROWS, HD), lambda h: (0, h)),
         ],
         out_specs=head_spec(MROWS),
         out_shape=jax.ShapeDtypeStruct((LANES, KVH, MROWS, HD), BF),
         scratch_shapes=[pltpu.VMEM((ROWS, HD), F32)],
         name="pack_query",
-    )(codes, queries, keys, weight)
+    )(codes, queries, keys)
 
 
 def pack_grad(codes, grads):
@@ -140,31 +142,100 @@
         grid=(4,),
         in_specs=[pl.BlockSpec((ROUNDS, 1024), lambda q: (0, q))],
         out_specs=pl.BlockSpec((PEERS, ROUNDS, 128), lambda q: (0, 0, q)),
-        out_shape=jax.ShapeDtypeStruct((PEERS, ROUNDS, 512), BF),
+        out_shape=jax.ShapeDtypeStruct((PEERS, ROUNDS, FEATS), BF),
         scratch_shapes=[pltpu.VMEM((1024, 1024), BF)],
         name="split_features",
     )(rows)
 
 
-def join_kernel(x_ref, out_ref, mix_ref):
+def smem():
+    return pl.BlockSpec(memory_space=pltpu.SMEM)
+
+
+def weight_kernel(where_ref, same_ref, other_ref, out_ref):
+    core = where_ref[4]
+    for x in range(4):
+        for z in range(8):
+            spot = (z // 2) * 8 + where_ref[x] * 2
+            out_ref[z % 2, spot + core] = same_ref[x, z]
+            out_ref[z % 2, spot + 1 - core] = other_ref[x, z]
+
+
+def weight_rows(where, same, other):
+    return pl.pallas_call(
+        weight_kernel,
+        in_specs=[smem()] + [pl.BlockSpec(memory_space=pltpu.VMEM)] * 2,
+        out_specs=pl.BlockSpec(memory_space=pltpu.VMEM),
+        out_shape=jax.ShapeDtypeStruct((2, LANES, WROWS, KVH * HD), BF),
+        name="weight_rows",
+    )(where, same, other)
+
+
+def values_kernel(peer_ref, x_ref, *refs):
+    out_ref = refs[RING]
+    total = jnp.zeros((ROUNDS, KVH * HD), F32)
+    for j in range(RING):
+        for z in range(2):
+            total = total + jnp.dot(
+                x_ref[z * RING + peer_ref[j]], refs[j][z], preferred_element_type=F32
+            )
+    out_ref[...] = total.astype(BF)
+
+
+def make_values(peers, split, parts):
+    return pl.pallas_call(
+        values_kernel,
+        in_specs=[smem()] + [pl.BlockSpec(memory_space=pltpu.VMEM)] * (1 + RING),
+        out_specs=pl.BlockSpec(memory_space=pltpu.VMEM),
+        out_shape=jax.ShapeDtypeStruct((ROUNDS, KVH * HD), BF),
+        name="make_values",
+    )(peers, split, *parts)
+
+
+def input_kernel(peer_ref, dv_ref, *refs):
+    out_ref, mix_ref, row_ref = refs[RING:]
+
     @pl.when(pl.program_id(0) == 0)
     def _():
         mix_ref[...] = mix_matrix(True)
 
-    parts = jnp.concatenate([x_ref[f] for f in range(PEERS)], axis=1)
-    out_ref[...] = jnp.dot(parts, mix_ref[...], preferred_element_type=F32).astype(BF)
-
-
-def join_features(parts):
-    return pl.pallas_call(
-        join_kernel,
+    for j in range(RING):
+        for z in range(2):
+            part = lax.dot_general(
+                dv_ref[...], refs[j][z], (((1,), (1,)), ((), ())), preferred_element_type=F32
+            )
+            lane = pl.multiple_of((z * RING + peer_ref[j]) * 128, 128)
+            row_ref[:, pl.ds(lane, 128)] = part.astype(BF)
+    out_ref[...] = jnp.dot(row_ref[...], mix_ref[...], preferred_element_type=F32).astype(BF)
+
+
+def make_input(peers, value_home, parts):
+    return pl.pallas_call(
+        input_kernel,
         grid=(4,),
-        in_specs=[pl.BlockSpec((PEERS, ROUNDS, 128), lambda q: (0, 0, q))],
+        in_specs=[smem(), pl.BlockSpec((ROUNDS, KVH * HD), lambda q: (0, 0))]
+        + [pl.BlockSpec((2, 128, KVH * HD), lambda q: (0, q, 0))] * RING,
         out_specs=pl.BlockSpec((ROUNDS, 1024), lambda q: (0, q)),
         out_shape=jax.ShapeDtypeStruct((ROUNDS, 4096), BF),
-        scratch_shapes=[pltpu.VMEM((1024, 1024), BF)],
-        name="join_features",
-    )(parts)
+        scratch_shapes=[pltpu.VMEM((1024, 1024), BF), pltpu.VMEM((ROUNDS, 1024), BF)],
+        name="make_input",
+    )(peers, value_home, *parts)
+
+
+def token_kernel(source_ref, *refs):
+    out_ref = refs[PEERS]
+    for j in range(PEERS):
+        out_ref[source_ref[j]] = refs[j][...]
+
+
+def token_rows_of(sources, parts):
+    return pl.pallas_call(
+        token_kernel,
+        in_specs=[smem()] + [pl.BlockSpec(memory_space=pltpu.VMEM)] * PEERS,
+        out_specs=pl.BlockSpec(memory_space=pltpu.VMEM),
+        out_shape=jax.ShapeDtypeStruct((PEERS, ROUNDS, FEATS), BF),
+        name="token_rows_of",
+    )(sources, *parts)
 
 
 def doc_table(slot, doc_ref):
@@ -175,7 +246,7 @@
 
 
 def own_keys(block_ref):
-    return block_ref[:, 0, HROWS + WROWS :].astype(F32).reshape(KEYS, HD).astype(BF)
+    return block_ref[:, 0, HROWS:].astype(F32).reshape(KEYS, HD).astype(BF)
 
 
 def probs_kernel(doc_ref, own_ref, p_ref, bias_ref):
@@ -281,7 +352,7 @@
 
 
 def body(inputs, queries, rotated_keys, out_grad, value_weight, fisher, anchor, doc_starts, owners):
-    own_lane = lax.axis_index("seq")
+    own_lane = lax.axis_index(SEQ)
     token_rows = inputs.reshape(ROUNDS, -1)
     query_rows = queries.reshape(ROUNDS, -1)
     key_rows = rotated_keys.reshape(ROUNDS, -1)
@@ -302,39 +373,55 @@
             pick, slots.reshape(KEYS, -1), (((0,), (0,)), ((), ())), preferred_element_type=F32
         ).astype(BF)
 
-    own = exchange(pack_query(codes, query_rows, key_rows, value_weight), "seq")
+    x, core, zl, y = (lax.axis_index(name) for name in ("x", "core", "zl", "y"))
+    steps = jnp.arange(4, dtype=jnp.int32)
+    where = jnp.concatenate([(x - steps) % 4, core[None]])
+    peers = (y - steps) % 4
+    peer = zl * RING + y
+    sources = (peer - jnp.arange(PEERS, dtype=jnp.int32)) % PEERS
+
+    def around(value, axis):
+        return [value] + [
+            lax.ppermute(value, axis, [(i, (i + k) % 4) for i in range(4)])
+            for k in (1, 2, 3)
+        ]
+
+    column = exchange(jnp.broadcast_to(value_weight[None], (8,) + value_weight.shape), ("zh", "zl"))
+    query_split = pack_query(codes, query_rows, key_rows)
     token_split = split_features(token_rows)
+    query_split, column = lax.optimization_barrier((query_split, column))
+    plane = jnp.stack(around(column, "x"))
+    other = lax.ppermute(plane, "core", [(0, 1), (1, 0)])
+    weight_part = weight_rows(where, plane, other).reshape(2, FEATS, -1)
+    weight_parts = around(weight_part, "y")
+
+    own = exchange(query_split, SEQ)
     grad_split = pack_grad(codes, grad_rows)
-    token_split, own = lax.optimization_barrier((token_split, own))
-    token_part = exchange(token_split, "fsdp").reshape(PEERS * ROUNDS, -1)
+    grad_split, own = lax.optimization_barrier((grad_split, own))
+    grad_own = exchange(grad_split, SEQ)
     probs = attend_probs(slot_doc, own)
-    weight_part = own[:, :, HROWS : HROWS + WROWS].transpose(0, 2, 1, 3).reshape(LANES * WROWS, -1)
-    grad_split, token_part = lax.optimization_barrier((grad_split, token_part))
-    grad_own = exchange(grad_split, "seq")
-    value_part = jnp.dot(token_part, weight_part, preferred_element_type=F32).astype(BF)
-    value_part, grad_own = lax.optimization_barrier((value_part, grad_own))
-    value_parts = exchange(value_part.reshape(PEERS, ROUNDS, -1), "fsdp")
+    tokens = []
+    for k in range(PEERS):
+        piece = lax.dynamic_index_in_dim(token_split, (peer + k) % PEERS, 0, keepdims=False)
+        if k:
+            piece = lax.ppermute(piece, FEAT, [(i, (i + k) % PEERS) for i in range(PEERS)])
+        tokens.append(piece)
+    token_part = token_rows_of(sources, tokens).reshape(PEERS * ROUNDS, -1)
+    values = make_values(peers, token_split, weight_parts)
     value_back = attend_value(probs, grad_own)
-    values = jnp.sum(value_parts.astype(F32), axis=0).astype(BF)
-
-    both = exchange(jnp.concatenate([place(values), value_back], axis=1), "seq")
+
+    both = exchange(jnp.concatenate([place(values), value_back], axis=1), SEQ)
     value_home = collect(both[:, CAP8:])
     value_all = exchange(
-        jnp.broadcast_to(value_home[None], (PEERS,) + value_home.shape), "fsdp"
+        jnp.broadcast_to(value_home[None], (PEERS,) + value_home.shape), FEAT
     ).reshape(PEERS * ROUNDS, -1)
     query_out, key_back = attend_query(probs, own, grad_own, both)
-
-    input_part = lax.dot_general(
-        value_all, weight_part, (((1,), (1,)), ((), ())), preferred_element_type=F32
-    ).astype(BF)
-    input_parts = exchange(input_part.reshape(PEERS, ROUNDS, -1), "fsdp")
+    input_grad = make_input(peers, value_home, weight_parts)
+
     weight_grad = lax.dot_general(
         token_part, value_all, (((0,), (0,)), ((), ())), preferred_element_type=F32
     ).astype(BF)
-    back = jnp.concatenate([weight_grad.reshape(LANES, WROWS, -1), key_back], axis=1)
-    back, input_parts = lax.optimization_barrier((back, input_parts))
-    last = exchange(back, "seq")
-    input_grad = join_features(input_parts)
+    last = exchange(jnp.concatenate([weight_grad.reshape(LANES, WROWS, -1), key_back], axis=1), SEQ)
     weight_sum = jnp.sum(last[:, :WROWS].astype(F32), axis=0)
     key_home = collect(last[:, WROWS:])
 
@@ -351,13 +438,14 @@
 
 
 def solution(mesh):
-    rows = P("fsdp", None, "seq", None)
-    weights = P(("seq", "fsdp"), None)
-    plan = P("fsdp", None)
+    fine = Mesh(mesh.devices.reshape(4, 4, 2, 2, 4), ("zh", "x", "core", "zl", "y"))
+    rows = P(FEAT, None, SEQ, None)
+    weights = P(SEQ + FEAT, None)
+    plan = P(FEAT, None)
     return jax.shard_map(
         body,
-        mesh=mesh,
+        mesh=fine,
         in_specs=(rows, rows, rows, rows, weights, weights, weights, plan, plan),
-        out_specs=(P("fsdp", "seq", None, None, None), rows, rows, weights),
+        out_specs=(P(FEAT, SEQ, None, None, None), rows, rows, weights),
         check_vma=False,
     )

time: 254 us -> 284 us (1.12)
  the two profiles are of different devices: /device:TPU:33 before, /device:TPU:0 now
where the time goes in v2:
time: 284 us; the launch traced here: 281 us
  waiting for transfers between devices  130 us (46%)
  starting transfers between devices  60 us (21%)
  Pallas kernels  47.3 us (17%)
  blocking collectives  24.9 us (9%)
  local copies, waits for them, and re-layouts  7.35 us (3%)
  other arithmetic  7.31 us (3%)
  matrix products  2.96 us (1%)
    all_to_all x5, waiting for transfers between devices, exchange(): return lax.all_to_all(value, axes, split_axis=0, concat_axis=0, tiled=True)  60.2 us
    ppermute x6, waiting for transfers between devices, around(): lax.ppermute(value, axis, [(i, (i + k) % 4) for i in range(4)])  48.2 us
    all_to_all x5, starting transfers between devices, exchange(): return lax.all_to_all(value, axes, split_axis=0, concat_axis=0, tiled=True)  36 us
    all_to_all x1, blocking collectives, exchange(): return lax.all_to_all(value, axes, split_axis=0, concat_axis=0, tiled=True)  24.9 us
    ppermute x7, waiting for transfers between devices, body(): lax.ppermute(piece, FEAT, [(i, (i + k) % PEERS) for i in range(PEERS)])  20.2 us
    ppermute x7, starting transfers between devices, body(): lax.ppermute(piece, FEAT, [(i, (i + k) % PEERS) for i in range(PEERS)])  12 us
    ppermute x6, starting transfers between devices, around(): lax.ppermute(value, axis, [(i, (i + k) % 4) for i in range(4)])  11.8 us
    pallas_call x1, Pallas kernels, attend_query(): pl.pallas_call(query_kernel, grid=(KVH,), in_specs=[probs_spec(), head_sp...  8.94 us
  transfers between devices with their start and end apart: 19, of which 11 were waited for; matrix products, arithmetic and copies ran while one was open for 2% of the time, Pallas kernels for 15%

profile of v2, /device:TPU:0, one launch (start us, length us, event | category | flops | bytes accessed | tf_op | source)
XLA Modules:
  0.0 280.7 jit_solution(7342531463246960053)
XLA Ops:
  0.6 1.4 broadcast_in_dim.20
  2.0 6.8 %all-to-all-start = ((bf16[8,16,512]{2,1,0:T(8,128)(2,1)}), bf16[8,16,512]{2,1,0:T(8,128)(2,1)S(1)}, u32[]{:S(2)}, u32[]{:S(2)}) async-start(bf16[8,16,512]{2,1,0:T(8,128)(2,1)} %broadcast_in_dim.20), calls=%async_computation | async-start | bytes 262144 | tf_op jit(solution)/shard_map/all_to_all | solution.py:38
  8.8 0.7 fusion.12
  9.4 0.1 convert_reduce_fusion.2
  9.5 0.7 select_reduce_fusion
  10.3 0.2 convert_reduce_fusion.1
  10.5 0.6 pad_add_fusion.code_ref
  11.1 4.4 %pack_query.1 = bf16[32,4,56,128]{3,2,1,0:T(8,128)(2,1)} custom-call(s32[2,128]{1,0:T(2,128)} %pad_add_fusion.code_ref, bf16[128,4096]{1,0:T(8,128)(2,1)} %bitcast.65, bf16[128,512]{1,0:T(8,128)(2,1)} %bitcast.70), custom_call_target="tpu_custom_call" | custom-call | tf_op jit(solution)/shard_map/pack_query/pallas_call | solution.py:95
  15.5 2.4 all-to-all-done
  17.9 7.7 %all-to-all-start.1 = ((bf16[32,4,56,128]{3,2,1,0:T(8,128)(2,1)}), bf16[32,4,56,128]{3,2,1,0:T(8,128)(2,1)S(1)}, u32[]{:S(2)}, u32[]{:S(2)}) async-start(bf16[32,4,56,128]{3,2,1,0:T(8,128)(2,1)} %pack_query.1), calls=%async_computation.1 | async-start | bytes 3670016 | tf_op jit(solution)/shard_map/all_to_all | solution.py:38
  25.5 4.2 %pack_grad.1 = bf16[32,4,48,128]{3,2,1,0:T(8,128)(2,1)} custom-call(s32[2,128]{1,0:T(2,128)} %pad_add_fusion.code_ref, bf16[128,4096]{1,0:T(8,128)(2,1)} %bitcast.64), custom_call_target="tpu_custom_call" | custom-call | tf_op jit(solution)/shard_map/pack_grad/pallas_call | solution.py:111
  29.7 40.6 %all-to-all-done.1.own_ref = bf16[32,4,56,128]{3,2,1,0:T(8,128)(2,1)S(1)} async-done(((bf16[32,4,56,128]{3,2,1,0:T(8,128)(2,1)}), bf16[32,4,56,128]{3,2,1,0:T(8,128)(2,1)S(1)}, u32[]{:S(2)}, u32[]{:S(2)}) %all-to-all-start.1) | async-done | bytes 1835040 | tf_op jit(solution)/shard_map/all_to_all | solution.py:38
  70.4 1.2 copy-done
  71.6 6.9 %all-to-all-start.2 = ((bf16[32,4,48,128]{3,2,1,0:T(8,128)(2,1)}), bf16[32,4,48,128]{3,2,1,0:T(8,128)(2,1)S(1)}, u32[]{:S(2)}, u32[]{:S(2)}) async-start(bf16[32,4,48,128]{3,2,1,0:T(8,128)(2,1)} %pack_grad.1), calls=%async_computation.2 | async-start | bytes 3145728 | tf_op jit(solution)/shard_map/all_to_all | solution.py:38
  78.6 1.9 collective-permute-start
  80.4 2.7 collective-permute-start.1
  83.1 1.5 collective-permute-start.2
  84.6 5.9 %collective-permute-done = bf16[8,16,512]{2,1,0:T(8,128)(2,1)S(1)} collective-permute-done((bf16[8,16,512]{2,1,0:T(8,128)(2,1)S(1)}, bf16[8,16,512]{2,1,0:T(8,128)(2,1)S(1)}, u32[]{:S(2)}, u32[]{:S(2)}) %collective-permute-start) | collective-permute-done | bytes 131104 | tf_op jit(solution)/shard_map/ppermute | solution.py:385
  90.5 3.6 %collective-permute-done.1 = bf16[8,16,512]{2,1,0:T(8,128)(2,1)S(1)} collective-permute-done((bf16[8,16,512]{2,1,0:T(8,128)(2,1)S(1)}, bf16[8,16,512]{2,1,0:T(8,128)(2,1)S(1)}, u32[]{:S(2)}, u32[]{:S(2)}) %collective-permute-start.1) | collective-permute-done | bytes 131104 | tf_op jit(solution)/shard_map/ppermute | solution.py:385
  94.3 0.6 pad_add_fusion.1.where_ref
  94.9 1.3 collective-permute-done.3.other_ref
  96.2 0.8 copy-done.8
  97.0 2.3 weight_rows.1
  99.2 1.6 collective-permute-start.4
  100.8 2.9 %collective-permute-start.5 = (bf16[2,512,512]{2,1,0:T(8,128)(2,1)}, bf16[2,512,512]{2,1,0:T(8,128)(2,1)}, u32[]{:S(2)}, u32[]{:S(2)}) collective-permute-start(bf16[2,512,512]{2,1,0:T(8,128)(2,1)} %bitcast.60), channel_id=1, source_target_pairs={{0,2},{1,3},{2,0},{3,1},{4,6},{5,7},{6,4},{7,5},{8,10},{9,11},{10,... | collective-permute-start | bytes 3145736 | tf_op jit(solution)/shard_map/ppermute | solution.py:385
  103.7 1.3 collective-permute-start.6
  105.1 4.7 %split_features.1.x_ref = bf16[8,128,512]{2,1,0:T(8,128)(2,1)} custom-call(bf16[128,4096]{1,0:T(8,128)(2,1)} %bitcast.66), custom_call_target="tpu_custom_call" | custom-call | tf_op jit(solution)/shard_map/split_features/pallas_call | solution.py:140
  109.8 0.5 and_select_fusion.2.peer_ref
  110.3 0.1 select_reduce_fusion.1
  110.4 0.5 broadcast_add_fusion.doc_ref
  111.0 15.0 %collective-permute-done.4.refs_1_ = bf16[2,512,512]{2,1,0:T(8,128)(2,1)S(1)} collective-permute-done((bf16[2,512,512]{2,1,0:T(8,128)(2,1)}, bf16[2,512,512]{2,1,0:T(8,128)(2,1)S(1)}, u32[]{:S(2)}, u32[]{:S(2)}) %collective-permute-start.4) | collective-permute-done | bytes 1048608 | tf_op jit(solution)/shard_map/ppermute | solution.py:385
  125.9 23.8 %collective-permute-done.5.refs_2_ = bf16[2,512,512]{2,1,0:T(8,128)(2,1)} collective-permute-done((bf16[2,512,512]{2,1,0:T(8,128)(2,1)}, bf16[2,512,512]{2,1,0:T(8,128)(2,1)}, u32[]{:S(2)}, u32[]{:S(2)}) %collective-permute-start.5) | collective-permute-done | bytes 1048608 | tf_op jit(solution)/shard_map/ppermute | solution.py:385
  149.7 3.9 %make_values.1 = bf16[128,512]{1,0:T(8,128)(2,1)} custom-call(s32[4]{0:T(128)} %and_select_fusion.2.peer_ref, bf16[8,128,512]{2,1,0:T(8,128)(2,1)} %split_features.1.x_ref, bf16[2,512,512]{2,1,0:T(8,128)(2,1)} %bitcast.62, bf16[2,512,512]{2,1,0:T(8,128)(2,1)} %copy-done.3, bf16[2,512,512]{2,1,0:T(8,128)(2,1)} %collective-permute-done.5.refs_2_, ...), custom_call_target="tpu_custom_call" | custom-call | tf_op jit(solution)/shard_map/make_values/pallas_call | solution.py:186
  153.6 1.1 fusion.1
  154.7 5.6 %attend_probs.1.p_ref = bf16[4,1536,256]{2,1,0:T(8,128)(2,1)} custom-call(s32[8]{0:T(128)} %broadcast_add_fusion.doc_ref, bf16[32,4,56,128]{3,2,1,0:T(8,128)(2,1)} %copy-done), custom_call_target="tpu_custom_call" | custom-call | tf_op jit(solution)/shard_map/attend_probs/pallas_call | solution.py:281
  160.3 1.2 copy-done.1
  161.5 4.6 %attend_value.1 = bf16[32,8,512]{2,1,0:T(8,128)(2,1)} custom-call(bf16[4,1536,256]{2,1,0:T(8,128)(2,1)} %attend_probs.1.p_ref, bf16[32,4,48,128]{3,2,1,0:T(8,128)(2,1)} %copy-done.1), custom_call_target="tpu_custom_call" | custom-call | tf_op jit(solution)/shard_map/attend_value/pallas_call | solution.py:301
  166.1 1.0 pad_maximum_fusion.2
  167.1 24.9 %all_to_all.30.v_ref = bf16[32,16,512]{2,1,0:T(8,128)(2,1)S(1)} all-to-all(bf16[32,16,512]{2,1,0:T(8,128)(2,1)S(1)} %pad_maximum_fusion.2), channel_id=1, replica_groups=mesh['zh'=4,'x'=4,'core'=2,'zl'=2,'y'=4] {'zh','x','core'}, dimensions={0} | all-to-all | bytes 1048576 | tf_op jit(solution)/shard_map/all_to_all | solution.py:38
  192.0 0.2 convolution_convert_fusion.2.dv_ref
  192.2 1.1 broadcast_in_dim.22
  193.3 10.8 %all-to-all-start.4 = ((bf16[8,128,512]{2,1,0:T(8,128)(2,1)}), bf16[8,128,512]{2,1,0:T(8,128)(2,1)S(1)}, u32[]{:S(2)}, u32[]{:S(2)}) async-start(bf16[8,128,512]{2,1,0:T(8,128)(2,1)} %broadcast_in_dim.22), calls=%async_computation.4 | async-start | bytes 2097152 | tf_op jit(solution)/shard_map/all_to_all | solution.py:38
  204.1 0.8 dynamic-slice_bitcast_fusion
  204.8 2.0 collective-permute-start.10
  206.8 1.5 collective-permute-start.11
  208.3 3.6 %collective-permute-start.12 = (bf16[128,512]{1,0:T(8,128)(2,1)S(1)}, bf16[128,512]{1,0:T(8,128)(2,1)S(1)}, u32[]{:S(2)}, u32[]{:S(2)}) collective-permute-start(bf16[128,512]{1,0:T(8,128)(2,1)S(1)} %get-tuple-element.17), channel_id=1, source_target_pairs={{0,6},{1,7},{2,0},{3,1},{4,2},{5,3},{6,4},{7,5},{8,14},{9,15},{10,... | collective-permute-start | bytes 393224 | tf_op jit(solution)/shard_map/ppermute | solution.py:407
  211.9 1.5 collective-permute-start.13
  213.3 0.6 collective-permute-start.7
  213.9 8.1 %collective-permute-done.10.refs_4_ = bf16[128,512]{1,0:T(8,128)(2,1)S(1)} collective-permute-done((bf16[128,512]{1,0:T(8,128)(2,1)S(1)}, bf16[128,512]{1,0:T(8,128)(2,1)S(1)}, u32[]{:S(2)}, u32[]{:S(2)}) %collective-permute-start.10) | collective-permute-done | bytes 131104 | tf_op jit(solution)/shard_map/ppermute | solution.py:407
  222.0 3.0 %collective-permute-start.8 = (bf16[128,512]{1,0:T(8,128)(2,1)S(1)}, bf16[128,512]{1,0:T(8,128)(2,1)S(1)}, u32[]{:S(2)}, u32[]{:S(2)}) collective-permute-start(bf16[128,512]{1,0:T(8,128)(2,1)S(1)} %get-tuple-element.21), channel_id=1, source_target_pairs={{0,2},{1,3},{2,4},{3,5},{4,6},{5,7},{6,0},{7,1},{8,10},{9,11},{10,... | collective-permute-start | bytes 393224 | tf_op jit(solution)/shard_map/ppermute | solution.py:407
  224.9 6.4 %collective-permute-done.11.refs_5_ = bf16[128,512]{1,0:T(8,128)(2,1)S(1)} collective-permute-done((bf16[128,512]{1,0:T(8,128)(2,1)S(1)}, bf16[128,512]{1,0:T(8,128)(2,1)S(1)}, u32[]{:S(2)}, u32[]{:S(2)}) %collective-permute-start.11) | collective-permute-done | bytes 131104 | tf_op jit(solution)/shard_map/ppermute | solution.py:407
  231.4 0.5 and_select_fusion.source_ref
  232.0 5.7 %collective-permute-done.9.refs_3_ = bf16[128,512]{1,0:T(8,128)(2,1)S(1)} collective-permute-done((bf16[128,512]{1,0:T(8,128)(2,1)S(1)}, bf16[128,512]{1,0:T(8,128)(2,1)S(1)}, u32[]{:S(2)}, u32[]{:S(2)}) %collective-permute-start.9) | collective-permute-done | bytes 131104 | tf_op jit(solution)/shard_map/ppermute | solution.py:407
  237.7 0.6 copy-done.16
  238.3 2.3 token_rows_of.1
  240.6 8.9 %attend_query.1 = (bf16[6,32,4096]{2,1,0:T(8,128)(2,1)}, bf16[32,8,512]{2,1,0:T(8,128)(2,1)}) custom-call(bf16[4,1536,256]{2,1,0:T(8,128)(2,1)} %attend_probs.1.p_ref, bf16[32,4,56,128]{3,2,1,0:T(8,128)(2,1)} %copy-done, bf16[32,4,48,128]{3,2,1,0:T(8,128)(2,1)} %copy-done.1, bf16[32,16,512]{2,1,0:T(8,128)(2,1)} %copy-done.4), custom_call_target="tpu_custom_call" | custom-call | tf_op jit(solution)/shard_map/attend_query/pallas_call | solution.py:340
  249.6 0.7 fusion
  250.3 0.2 copy-done.9
  250.5 1.0 pad_maximum_fusion
  251.5 3.9 %all-to-all-start.5 = ((bf16[32,24,512]{2,1,0:T(8,128)(2,1)}), bf16[32,24,512]{2,1,0:T(8,128)(2,1)S(1)}, u32[]{:S(2)}, u32[]{:S(2)}) async-start(bf16[32,24,512]{2,1,0:T(8,128)(2,1)} %pad_maximum_fusion), calls=%async_computation.5 | async-start | bytes 1572864 | tf_op jit(solution)/shard_map/all_to_all | solution.py:38
  255.4 6.4 %make_input.1 = bf16[128,4096]{1,0:T(8,128)(2,1)} custom-call(s32[4]{0:T(128)} %and_select_fusion.2.peer_ref, bf16[128,512]{1,0:T(8,128)(2,1)} %copy-done.6, bf16[2,512,512]{2,1,0:T(8,128)(2,1)} %bitcast.63, bf16[2,512,512]{2,1,0:T(8,128)(2,1)} %copy-done.3, bf16[2,512,512]{2,1,0:T(8,128)(2,1)} %collective-permute-done.5.refs_2_, ...), custom_call_target="tpu_custom_call" | custom-call | tf_op jit(solution)/shard_map/make_input/pallas_call | solution.py:213
  261.8 17.2 %all-to-all-done.5 = bf16[32,24,512]{2,1,0:T(8,128)(2,1)S(1)} async-done(((bf16[32,24,512]{2,1,0:T(8,128)(2,1)}), bf16[32,24,512]{2,1,0:T(8,128)(2,1)S(1)}, u32[]{:S(2)}, u32[]{:S(2)}) %all-to-all-start.5) | async-done | bytes 786464 | tf_op jit(solution)/shard_map/all_to_all | solution.py:38
  279.1 0.6 multiply_add_fusion
  279.8 0.9 fusion.2
  (52 shorter events, 0.4 us)
Async XLA Ops:
  2.0 15.9 %all-to-all-start = ((bf16[8,16,512]{2,1,0:T(8,128)(2,1)}), bf16[8,16,512]{2,1,0:T(8,128)(2,1)S(1)}, u32[]{:S(2)}, u32[]{:S(2)}) async-start(bf16[8,16,512]{2,1,0:T(8,128)(2,1)} %broadcast_in_dim.20), calls=%async_computation | async-start | bytes 262144 | tf_op jit(solution)/shard_map/all_to_all | solution.py:38
  17.9 52.5 %all-to-all-start.1 = ((bf16[32,4,56,128]{3,2,1,0:T(8,128)(2,1)}), bf16[32,4,56,128]{3,2,1,0:T(8,128)(2,1)S(1)}, u32[]{:S(2)}, u32[]{:S(2)}) async-start(bf16[32,4,56,128]{3,2,1,0:T(8,128)(2,1)} %pack_query.1), calls=%async_computation.1 | async-start | bytes 3670016 | tf_op jit(solution)/shard_map/all_to_all | solution.py:38
  70.4 1.2 copy-start
  71.6 88.7 %all-to-all-start.2 = ((bf16[32,4,48,128]{3,2,1,0:T(8,128)(2,1)}), bf16[32,4,48,128]{3,2,1,0:T(8,128)(2,1)S(1)}, u32[]{:S(2)}, u32[]{:S(2)}) async-start(bf16[32,4,48,128]{3,2,1,0:T(8,128)(2,1)} %pack_grad.1), calls=%async_computation.2 | async-start | bytes 3145728 | tf_op jit(solution)/shard_map/all_to_all | solution.py:38
  78.6 11.9 %collective-permute-start = (bf16[8,16,512]{2,1,0:T(8,128)(2,1)S(1)}, bf16[8,16,512]{2,1,0:T(8,128)(2,1)S(1)}, u32[]{:S(2)}, u32[]{:S(2)}) collective-permute-start(bf16[8,16,512]{2,1,0:T(8,128)(2,1)S(1)} %all-to-all-done), channel_id=1, source_target_pairs={{0,16},{16,32},{32,48},{48,0},{1,17},{17,33},{33,49},{49,1},{2,18}... | collective-permute-start | bytes 393224 | tf_op jit(solution)/shard_map/ppermute | solution.py:385
  80.4 13.6 %collective-permute-start.1 = (bf16[8,16,512]{2,1,0:T(8,128)(2,1)S(1)}, bf16[8,16,512]{2,1,0:T(8,128)(2,1)S(1)}, u32[]{:S(2)}, u32[]{:S(2)}) collective-permute-start(bf16[8,16,512]{2,1,0:T(8,128)(2,1)S(1)} %all-to-all-done), channel_id=1, source_target_pairs={{0,32},{16,48},{32,0},{48,16},{1,33},{17,49},{33,1},{49,17},{2,34}... | collective-permute-start | bytes 393224 | tf_op jit(solution)/shard_map/ppermute | solution.py:385
  83.1 11.0 %collective-permute-start.2 = (bf16[8,16,512]{2,1,0:T(8,128)(2,1)S(1)}, bf16[8,16,512]{2,1,0:T(8,128)(2,1)S(1)}, u32[]{:S(2)}, u32[]{:S(2)}) collective-permute-start(bf16[8,16,512]{2,1,0:T(8,128)(2,1)S(1)} %all-to-all-done), channel_id=1, source_target_pairs={{0,48},{16,0},{32,16},{48,32},{1,49},{17,1},{33,17},{49,33},{2,50}... | collective-permute-start | bytes 393224 | tf_op jit(solution)/shard_map/ppermute | solution.py:385
  94.1 2.0 copy-start.5
  94.1 2.0 collective-permute-start.3
  96.1 0.8 copy-start.8
  99.2 26.7 %collective-permute-start.4 = (bf16[2,512,512]{2,1,0:T(8,128)(2,1)}, bf16[2,512,512]{2,1,0:T(8,128)(2,1)S(1)}, u32[]{:S(2)}, u32[]{:S(2)}) collective-permute-start(bf16[2,512,512]{2,1,0:T(8,128)(2,1)} %bitcast.59), channel_id=1, source_target_pairs={{0,1},{1,2},{2,3},{3,0},{4,5},{5,6},{6,7},{7,4},{8,9},{9,10},{10,1... | collective-permute-start | bytes 3145736 | tf_op jit(solution)/shard_map/ppermute | solution.py:385
  100.8 48.9 %collective-permute-start.5 = (bf16[2,512,512]{2,1,0:T(8,128)(2,1)}, bf16[2,512,512]{2,1,0:T(8,128)(2,1)}, u32[]{:S(2)}, u32[]{:S(2)}) collective-permute-start(bf16[2,512,512]{2,1,0:T(8,128)(2,1)} %bitcast.60), channel_id=1, source_target_pairs={{0,2},{1,3},{2,0},{3,1},{4,6},{5,7},{6,4},{7,5},{8,10},{9,11},{10,... | collective-permute-start | bytes 3145736 | tf_op jit(solution)/shard_map/ppermute | solution.py:385
  103.7 46.0 %collective-permute-start.6 = (bf16[2,512,512]{2,1,0:T(8,128)(2,1)}, bf16[2,512,512]{2,1,0:T(8,128)(2,1)}, u32[]{:S(2)}, u32[]{:S(2)}) collective-permute-start(bf16[2,512,512]{2,1,0:T(8,128)(2,1)} %bitcast.61), channel_id=1, source_target_pairs={{0,3},{1,0},{2,1},{3,2},{4,7},{5,4},{6,5},{7,6},{8,11},{9,8},{10,9... | collective-permute-start | bytes 3145736 | tf_op jit(solution)/shard_map/ppermute | solution.py:385
  125.9 23.8 %copy-start.3 = (bf16[2,512,512]{2,1,0:T(8,128)(2,1)}, bf16[2,512,512]{2,1,0:T(8,128)(2,1)S(1)}, u32[]{:S(2)}) copy-start(bf16[2,512,512]{2,1,0:T(8,128)(2,1)S(1)} %collective-permute-done.4.refs_1_) | copy-start | bytes 3145732
  160.3 1.2 copy-start.1
  192.0 1.3 copy-start.4
  192.2 1.1 copy-start.6
  192.2 11.8 %copy-start.2 = (bf16[8,128,512]{2,1,0:T(8,128)(2,1)S(1)}, bf16[8,128,512]{2,1,0:T(8,128)(2,1)}, u32[]{:S(2)}) copy-start(bf16[8,128,512]{2,1,0:T(8,128)(2,1)} %split_features.1.x_ref) | copy-start | bytes 3145732
  193.3 56.3 %all-to-all-start.4 = ((bf16[8,128,512]{2,1,0:T(8,128)(2,1)}), bf16[8,128,512]{2,1,0:T(8,128)(2,1)S(1)}, u32[]{:S(2)}, u32[]{:S(2)}) async-start(bf16[8,128,512]{2,1,0:T(8,128)(2,1)} %broadcast_in_dim.22), calls=%async_computation.4 | async-start | bytes 2097152 | tf_op jit(solution)/shard_map/all_to_all | solution.py:38
  204.8 17.1 %collective-permute-start.10 = (bf16[128,512]{1,0:T(8,128)(2,1)S(1)}, bf16[128,512]{1,0:T(8,128)(2,1)S(1)}, u32[]{:S(2)}, u32[]{:S(2)}) collective-permute-start(bf16[128,512]{1,0:T(8,128)(2,1)S(1)} %get-tuple-element.19), channel_id=1, source_target_pairs={{0,4},{1,5},{2,6},{3,7},{4,0},{5,1},{6,2},{7,3},{8,12},{9,13},{10,... | collective-permute-start | bytes 393224 | tf_op jit(solution)/shard_map/ppermute | solution.py:407
  206.8 24.5 %collective-permute-start.11 = (bf16[128,512]{1,0:T(8,128)(2,1)S(1)}, bf16[128,512]{1,0:T(8,128)(2,1)S(1)}, u32[]{:S(2)}, u32[]{:S(2)}) collective-permute-start(bf16[128,512]{1,0:T(8,128)(2,1)S(1)} %get-tuple-element.18), channel_id=1, source_target_pairs={{0,5},{1,6},{2,7},{3,0},{4,1},{5,2},{6,3},{7,4},{8,13},{9,14},{10,... | collective-permute-start | bytes 393224 | tf_op jit(solution)/shard_map/ppermute | solution.py:407
  208.3 23.6 %collective-permute-start.12 = (bf16[128,512]{1,0:T(8,128)(2,1)S(1)}, bf16[128,512]{1,0:T(8,128)(2,1)S(1)}, u32[]{:S(2)}, u32[]{:S(2)}) collective-permute-start(bf16[128,512]{1,0:T(8,128)(2,1)S(1)} %get-tuple-element.17), channel_id=1, source_target_pairs={{0,6},{1,7},{2,0},{3,1},{4,2},{5,3},{6,4},{7,5},{8,14},{9,15},{10,... | collective-permute-start | bytes 393224 | tf_op jit(solution)/shard_map/ppermute | solution.py:407
  211.9 20.1 %collective-permute-start.13 = (bf16[128,512]{1,0:T(8,128)(2,1)S(1)}, bf16[128,512]{1,0:T(8,128)(2,1)S(1)}, u32[]{:S(2)}, u32[]{:S(2)}) collective-permute-start(bf16[128,512]{1,0:T(8,128)(2,1)S(1)} %get-tuple-element.16), channel_id=1, source_target_pairs={{0,7},{1,0},{2,1},{3,2},{4,3},{5,4},{6,5},{7,6},{8,15},{9,8},{10,9... | collective-permute-start | bytes 393224 | tf_op jit(solution)/shard_map/ppermute | solution.py:407
  213.3 18.6 %collective-permute-start.7 = (bf16[128,512]{1,0:T(8,128)(2,1)S(1)}, bf16[128,512]{1,0:T(8,128)(2,1)S(1)}, u32[]{:S(2)}, u32[]{:S(2)}) collective-permute-start(bf16[128,512]{1,0:T(8,128)(2,1)S(1)} %get-tuple-element.22), channel_id=1, source_target_pairs={{0,1},{1,2},{2,3},{3,4},{4,5},{5,6},{6,7},{7,0},{8,9},{9,10},{10,1... | collective-permute-start | bytes 393224 | tf_op jit(solution)/shard_map/ppermute | solution.py:407
  222.0 15.7 %copy-start.10 = (bf16[128,512]{1,0:T(8,128)(2,1)}, bf16[128,512]{1,0:T(8,128)(2,1)S(1)}, u32[]{:S(2)}) copy-start(bf16[128,512]{1,0:T(8,128)(2,1)S(1)} %collective-permute-done.10.refs_4_) | copy-start | bytes 393220
  222.0 10.0 %collective-permute-start.8 = (bf16[128,512]{1,0:T(8,128)(2,1)S(1)}, bf16[128,512]{1,0:T(8,128)(2,1)S(1)}, u32[]{:S(2)}, u32[]{:S(2)}) collective-permute-start(bf16[128,512]{1,0:T(8,128)(2,1)S(1)} %get-tuple-element.21), channel_id=1, source_target_pairs={{0,2},{1,3},{2,4},{3,5},{4,6},{5,7},{6,0},{7,1},{8,10},{9,11},{10,... | collective-permute-start | bytes 393224 | tf_op jit(solution)/shard_map/ppermute | solution.py:407
  231.4 6.3 %copy-start.11 = (bf16[128,512]{1,0:T(8,128)(2,1)}, bf16[128,512]{1,0:T(8,128)(2,1)S(1)}, u32[]{:S(2)}) copy-start(bf16[128,512]{1,0:T(8,128)(2,1)S(1)} %collective-permute-done.11.refs_5_) | copy-start | bytes 393220
  231.4 6.3 %collective-permute-start.9 = (bf16[128,512]{1,0:T(8,128)(2,1)S(1)}, bf16[128,512]{1,0:T(8,128)(2,1)S(1)}, u32[]{:S(2)}, u32[]{:S(2)}) collective-permute-start(bf16[128,512]{1,0:T(8,128)(2,1)S(1)} %get-tuple-element.20), channel_id=1, source_target_pairs={{0,3},{1,4},{2,5},{3,6},{4,7},{5,0},{6,1},{7,2},{8,11},{9,12},{10,... | collective-permute-start | bytes 393224 | tf_op jit(solution)/shard_map/ppermute | solution.py:407
  231.9 5.7 %copy-start.12 = (bf16[128,512]{1,0:T(8,128)(2,1)}, bf16[128,512]{1,0:T(8,128)(2,1)S(1)}, u32[]{:S(2)}) copy-start(bf16[128,512]{1,0:T(8,128)(2,1)S(1)} %collective-permute-done.12.refs_6_) | copy-start | bytes 393220
  231.9 5.7 %copy-start.13 = (bf16[128,512]{1,0:T(8,128)(2,1)}, bf16[128,512]{1,0:T(8,128)(2,1)S(1)}, u32[]{:S(2)}) copy-start(bf16[128,512]{1,0:T(8,128)(2,1)S(1)} %collective-permute-done.13.refs_7_) | copy-start | bytes 393220
  232.0 5.7 %copy-start.14 = (bf16[128,512]{1,0:T(8,128)(2,1)}, bf16[128,512]{1,0:T(8,128)(2,1)S(1)}, u32[]{:S(2)}) copy-start(bf16[128,512]{1,0:T(8,128)(2,1)S(1)} %collective-permute-done.7.refs_1_) | copy-start | bytes 393220
  232.0 5.7 %copy-start.15 = (bf16[128,512]{1,0:T(8,128)(2,1)}, bf16[128,512]{1,0:T(8,128)(2,1)S(1)}, u32[]{:S(2)}) copy-start(bf16[128,512]{1,0:T(8,128)(2,1)S(1)} %collective-permute-done.8.refs_2_) | copy-start | bytes 393220
  237.6 0.7 copy-start.16
  240.6 8.9 %copy-start.7 = (bf16[8,128,512]{2,1,0:T(8,128)(2,1)S(1)}, bf16[8,128,512]{2,1,0:T(8,128)(2,1)}, u32[]{:S(2)}) copy-start(bf16[8,128,512]{2,1,0:T(8,128)(2,1)} %token_rows_of.1) | copy-start | bytes 3145732
  249.6 0.9 copy-start.9
  251.5 27.5 %all-to-all-start.5 = ((bf16[32,24,512]{2,1,0:T(8,128)(2,1)}), bf16[32,24,512]{2,1,0:T(8,128)(2,1)S(1)}, u32[]{:S(2)}, u32[]{:S(2)}) async-start(bf16[32,24,512]{2,1,0:T(8,128)(2,1)} %pad_maximum_fusion), calls=%async_computation.5 | async-start | bytes 1572864 | tf_op jit(solution)/shard_map/all_to_all | solution.py:38
  255.4 23.7 %copy-start.17 = (bf16[16,512]{1,0:T(8,128)(2,1)S(1)}, bf16[16,512]{1,0:T(8,128)(2,1)}, u32[]{:S(2)}) copy-start(bf16[16,512]{1,0:T(8,128)(2,1)} %param.13) | copy-start | bytes 49156
  255.4 23.7 %copy-start.18 = (f32[16,512]{1,0:T(8,128)S(1)}, f32[16,512]{1,0:T(8,128)}, u32[]{:S(2)}) copy-start(f32[16,512]{1,0:T(8,128)} %param.15) | copy-start | bytes 98308
  255.4 23.7 %copy-start.19 = (f32[16,512]{1,0:T(8,128)S(1)}, f32[16,512]{1,0:T(8,128)}, u32[]{:S(2)}) copy-start(f32[16,512]{1,0:T(8,128)} %param.14) | copy-start | bytes 98308

commit v3 on v2

--- a/solution.py
+++ b/solution.py
@@ -91,6 +91,10 @@
     return pl.BlockSpec((1, ROWS, KEYS), lambda h: (h, 0, 0))
 
 
+def turned_spec():
+    return pl.BlockSpec((1, KEYS, ROWS), lambda h: (h, 0, 0))
+
+
 def pack_query(codes, queries, keys):
     return pl.pallas_call(
         pack_query_kernel,
@@ -171,25 +175,23 @@
     )(where, same, other)
 
 
-def values_kernel(peer_ref, x_ref, *refs):
-    out_ref = refs[RING]
-    total = jnp.zeros((ROUNDS, KVH * HD), F32)
-    for j in range(RING):
-        for z in range(2):
-            total = total + jnp.dot(
-                x_ref[z * RING + peer_ref[j]], refs[j][z], preferred_element_type=F32
-            )
-    out_ref[...] = total.astype(BF)
-
-
-def make_values(peers, split, parts):
-    return pl.pallas_call(
-        values_kernel,
-        in_specs=[smem()] + [pl.BlockSpec(memory_space=pltpu.VMEM)] * (1 + RING),
-        out_specs=pl.BlockSpec(memory_space=pltpu.VMEM),
-        out_shape=jax.ShapeDtypeStruct((ROUNDS, KVH * HD), BF),
-        name="make_values",
-    )(peers, split, *parts)
+def partial_kernel(w_ref, *refs):
+    parts, outs = refs[:RING], refs[RING:]
+    for part, out in zip(parts, outs):
+        total = jnp.dot(part[0], w_ref[0], preferred_element_type=F32)
+        total = total + jnp.dot(part[1], w_ref[1], preferred_element_type=F32)
+        out[...] = total.astype(BF)
+
+
+def partial_values(weight, parts):
+    whole = pl.BlockSpec(memory_space=pltpu.VMEM)
+    return pl.pallas_call(
+        partial_kernel,
+        in_specs=[whole] * (1 + RING),
+        out_specs=[whole] * RING,
+        out_shape=[jax.ShapeDtypeStruct((ROUNDS, KVH * HD), BF)] * RING,
+        name="partial_values",
+    )(weight, *parts)
 
 
 def input_kernel(peer_ref, dv_ref, *refs):
@@ -223,19 +225,22 @@
 
 
 def token_kernel(source_ref, *refs):
-    out_ref = refs[PEERS]
-    for j in range(PEERS):
-        out_ref[source_ref[j]] = refs[j][...]
-
-
-def token_rows_of(sources, parts):
+    out_ref = refs[RING + 1]
+    zl = source_ref[RING]
+    for j in range(RING):
+        out_ref[zl * RING + source_ref[j]] = refs[j][zl]
+        out_ref[(1 - zl) * RING + source_ref[j]] = refs[RING][j]
+
+
+def token_rows_of(sources, parts, crossed):
+    whole = pl.BlockSpec(memory_space=pltpu.VMEM)
     return pl.pallas_call(
         token_kernel,
-        in_specs=[smem()] + [pl.BlockSpec(memory_space=pltpu.VMEM)] * PEERS,
-        out_specs=pl.BlockSpec(memory_space=pltpu.VMEM),
+        in_specs=[smem()] + [whole] * (RING + 1),
+        out_specs=whole,
         out_shape=jax.ShapeDtypeStruct((PEERS, ROUNDS, FEATS), BF),
         name="token_rows_of",
-    )(sources, *parts)
+    )(sources, *parts, crossed)
 
 
 def doc_table(slot, doc_ref):
@@ -249,7 +254,7 @@
     return block_ref[:, 0, HROWS:].astype(F32).reshape(KEYS, HD).astype(BF)
 
 
-def probs_kernel(doc_ref, own_ref, p_ref, bias_ref):
+def probs_kernel(doc_ref, own_ref, p_ref, turned_ref, bias_ref):
     @pl.when(pl.program_id(0) == 0)
     def _():
         shape = (LANES, HROWS, KEYS)
@@ -274,7 +279,9 @@
         peak = jnp.max(scores, axis=1, keepdims=True)
         weight = jnp.exp(scores - peak)
         total = jnp.sum(weight, axis=1, keepdims=True)
-        p_ref[0, rows, :] = (weight * (1.0 / total)).astype(BF)
+        probs = weight * (1.0 / total)
+        p_ref[0, rows, :] = probs.astype(BF)
+        turned_ref[0, :, rows] = probs.T.astype(BF)
 
 
 def attend_probs(slot_doc, own):
@@ -282,30 +289,31 @@
         probs_kernel,
         grid=(KVH,),
         in_specs=[pl.BlockSpec(memory_space=pltpu.SMEM), head_spec(MROWS)],
-        out_specs=probs_spec(),
-        out_shape=jax.ShapeDtypeStruct((KVH, ROWS, KEYS), BF),
+        out_specs=(probs_spec(), turned_spec()),
+        out_shape=(
+            jax.ShapeDtypeStruct((KVH, ROWS, KEYS), BF),
+            jax.ShapeDtypeStruct((KVH, KEYS, ROWS), BF),
+        ),
         scratch_shapes=[pltpu.VMEM((ROWS, KEYS), F32)],
         name="attend_probs",
     )(slot_doc, own)
 
 
-def value_kernel(p_ref, g_ref, dv_ref):
+def value_kernel(p_ref, g_ref, v_ref, out_ref):
     grad = g_ref[...].reshape(ROWS, HD)
-    turned = lax.dot_general(
-        grad, p_ref[0], (((0,), (0,)), ((), ())), preferred_element_type=F32
-    )
-    dv_ref[...] = turned.T.astype(BF).reshape(LANES, CAP8, HD)
-
-
-def attend_value(probs, grad):
+    value_grad = jnp.dot(p_ref[0], grad, preferred_element_type=F32).reshape(LANES, CAP8, HD)
+    out_ref[...] = jnp.concatenate([v_ref[...].astype(F32), value_grad], axis=1).astype(BF)
+
+
+def attend_value(turned, grad, values):
     return pl.pallas_call(
         value_kernel,
         grid=(KVH,),
-        in_specs=[probs_spec(), head_spec(HROWS)],
-        out_specs=key_spec(),
-        out_shape=jax.ShapeDtypeStruct((LANES, CAP8, KVH * HD), BF),
+        in_specs=[turned_spec(), head_spec(HROWS), key_spec()],
+        out_specs=pl.BlockSpec((LANES, 2 * CAP8, HD), lambda h: (0, 0, h)),
+        out_shape=jax.ShapeDtypeStruct((LANES, 2 * CAP8, KVH * HD), BF),
         name="attend_value",
-    )(probs, grad)
+    )(turned, grad, values)
 
 
 def query_kernel(p_ref, own_ref, g_ref, v_ref, dq_ref, dk_ref, ds_ref, acc_ref):
@@ -377,8 +385,6 @@
     steps = jnp.arange(4, dtype=jnp.int32)
     where = jnp.concatenate([(x - steps) % 4, core[None]])
     peers = (y - steps) % 4
-    peer = zl * RING + y
-    sources = (peer - jnp.arange(PEERS, dtype=jnp.int32)) % PEERS
 
     def around(value, axis):
         return [value] + [
@@ -393,24 +399,35 @@
     plane = jnp.stack(around(column, "x"))
     other = lax.ppermute(plane, "core", [(0, 1), (1, 0)])
     weight_part = weight_rows(where, plane, other).reshape(2, FEATS, -1)
+    halves = token_split.reshape(2, RING, ROUNDS, FEATS)
+    tokens = []
+    for k in range(RING):
+        piece = lax.dynamic_index_in_dim(halves, (y + k) % RING, 1, keepdims=False)
+        if k:
+            piece = lax.ppermute(piece, "y", [(i, (i + k) % RING) for i in range(RING)])
+        tokens.append(piece)
+    shares = partial_values(weight_part, tokens)
+    values = shares[0].astype(F32)
+    for k in (1, 2, 3):
+        share = lax.ppermute(shares[k], "y", [(i, (i - k) % RING) for i in range(RING)])
+        values = values + share.astype(F32)
+    values = values.astype(BF)
     weight_parts = around(weight_part, "y")
 
     own = exchange(query_split, SEQ)
     grad_split = pack_grad(codes, grad_rows)
     grad_split, own = lax.optimization_barrier((grad_split, own))
     grad_own = exchange(grad_split, SEQ)
-    probs = attend_probs(slot_doc, own)
-    tokens = []
-    for k in range(PEERS):
-        piece = lax.dynamic_index_in_dim(token_split, (peer + k) % PEERS, 0, keepdims=False)
-        if k:
-            piece = lax.ppermute(piece, FEAT, [(i, (i + k) % PEERS) for i in range(PEERS)])
-        tokens.append(piece)
-    token_part = token_rows_of(sources, tokens).reshape(PEERS * ROUNDS, -1)
-    values = make_values(peers, token_split, weight_parts)
-    value_back = attend_value(probs, grad_own)
-
-    both = exchange(jnp.concatenate([place(values), value_back], axis=1), SEQ)
+    probs, turned = attend_probs(slot_doc, own)
+    crossed = jnp.stack(
+        [lax.dynamic_index_in_dim(part, 1 - zl, 0, keepdims=False) for part in tokens]
+    )
+    crossed = lax.ppermute(crossed, "zl", [(0, 1), (1, 0)])
+    token_part = token_rows_of(
+        jnp.concatenate([peers, zl[None]]), tokens, crossed
+    ).reshape(PEERS * ROUNDS, -1)
+
+    both = exchange(attend_value(turned, grad_own, place(values)), SEQ)
     value_home = collect(both[:, CAP8:])
     value_all = exchange(
         jnp.broadcast_to(value_home[None], (PEERS,) + value_home.shape), FEAT

time: 284 us -> 276 us (0.972)
  starting transfers between devices: 60 us -> 51.7 us
  waiting for transfers between devices: 130 us -> 125 us
  local copies, waits for them, and re-layouts: 7.35 us -> 11.7 us
    all_to_all x5, waiting for transfers between devices: 60.2 us -> 43.1 us  [exchange(): return lax.all_to_all(value, axes, split_axis=0, concat_axis=0, tiled=True)]
    ppermute x7, waiting for transfers between devices: 20.2 us -> 28.3 us  [the longest x1 21.7 us: body(): crossed = lax.ppermute(crossed, 'zl', [(0, 1), (1, 0)])]
    all_to_all x5, starting transfers between devices: 36 us -> 30.2 us  [exchange(): return lax.all_to_all(value, axes, split_axis=0, concat_axis=0, tiled=True)]
    ppermute x6, waiting for transfers between devices: 48.2 us -> 52.9 us  [around(): lax.ppermute(value, axis, [(i, (i + k) % 4) for i in range(4)])]
    unnamed x40 -> x44, local copies, waits for them, and re-layouts: 4.13 us -> 6.14 us
  transfers between devices with their start and end apart: 19 -> 19, of which waited for: 11 -> 11; matrix products, arithmetic and copies ran while one was open for 2% -> 3% of each run, Pallas kernels for 15% -> 16%
where the time goes in v3:
time: 276 us; the launch traced here: 273 us
  waiting for transfers between devices  125 us (45%)
  starting transfers between devices  51.7 us (19%)
  Pallas kernels  47.5 us (17%)
  blocking collectives  25.7 us (9%)
  local copies, waits for them, and re-layouts  11.7 us (4%)
  other arithmetic  5.9 us (2%)
  matrix products  3.72 us (1%)
    ppermute x6, waiting for transfers between devices, around(): lax.ppermute(value, axis, [(i, (i + k) % 4) for i in range(4)])  52.9 us
    all_to_all x5, waiting for transfers between devices, exchange(): return lax.all_to_all(value, axes, split_axis=0, concat_axis=0, tiled=True)  43.1 us
    all_to_all x5, starting transfers between devices, exchange(): return lax.all_to_all(value, axes, split_axis=0, concat_axis=0, tiled=True)  30.2 us
    all_to_all x1, blocking collectives, exchange(): return lax.all_to_all(value, axes, split_axis=0, concat_axis=0, tiled=True)  25.7 us
    ppermute x1, waiting for transfers between devices, body(): crossed = lax.ppermute(crossed, 'zl', [(0, 1), (1, 0)])  21.7 us
    ppermute x6, starting transfers between devices, around(): lax.ppermute(value, axis, [(i, (i + k) % 4) for i in range(4)])  10.4 us
    pallas_call x1, Pallas kernels, attend_query(): pl.pallas_call(query_kernel, grid=(KVH,), in_specs=[probs_spec(), head_sp...  8.94 us
    pallas_call x1, Pallas kernels, attend_probs(): pl.pallas_call(probs_kernel, grid=(KVH,), in_specs=[pl.BlockSpec(memory_s...  6.76 us
  transfers between devices with their start and end apart: 19, of which 11 were waited for; matrix products, arithmetic and copies ran while one was open for 3% of the time, Pallas kernels for 16%

profile of v3, /device:TPU:0, one launch (start us, length us, event | category | flops | bytes accessed | tf_op | source)
XLA Modules:
  0.0 272.7 jit_solution(5111031078215747862)
XLA Ops:
  0.6 1.4 broadcast_in_dim.22
  2.0 6.8 %all-to-all-start = ((bf16[8,16,512]{2,1,0:T(8,128)(2,1)}), bf16[8,16,512]{2,1,0:T(8,128)(2,1)S(1)}, u32[]{:S(2)}, u32[]{:S(2)}) async-start(bf16[8,16,512]{2,1,0:T(8,128)(2,1)} %broadcast_in_dim.22), calls=%async_computation | async-start | bytes 262144 | tf_op jit(solution)/shard_map/all_to_all | solution.py:38
  8.8 0.7 fusion.11
  9.5 0.7 select_reduce_fusion
  10.3 0.2 convert_reduce_fusion.1
  10.5 0.6 pad_add_fusion.code_ref
  11.1 4.4 %pack_query.1 = bf16[32,4,56,128]{3,2,1,0:T(8,128)(2,1)} custom-call(s32[2,128]{1,0:T(2,128)} %pad_add_fusion.code_ref, bf16[128,4096]{1,0:T(8,128)(2,1)} %bitcast.68, bf16[128,512]{1,0:T(8,128)(2,1)} %bitcast.73), custom_call_target="tpu_custom_call" | custom-call | tf_op jit(solution)/shard_map/pack_query/pallas_call | solution.py:99
  15.4 2.4 all-to-all-done
  17.9 7.6 %all-to-all-start.1 = ((bf16[32,4,56,128]{3,2,1,0:T(8,128)(2,1)}), bf16[32,4,56,128]{3,2,1,0:T(8,128)(2,1)S(1)}, u32[]{:S(2)}, u32[]{:S(2)}) async-start(bf16[32,4,56,128]{3,2,1,0:T(8,128)(2,1)} %pack_query.1), calls=%async_computation.1 | async-start | bytes 3670016 | tf_op jit(solution)/shard_map/all_to_all | solution.py:38
  25.5 4.2 %pack_grad.1 = bf16[32,4,48,128]{3,2,1,0:T(8,128)(2,1)} custom-call(s32[2,128]{1,0:T(2,128)} %pad_add_fusion.code_ref, bf16[128,4096]{1,0:T(8,128)(2,1)} %bitcast.67), custom_call_target="tpu_custom_call" | custom-call | tf_op jit(solution)/shard_map/pack_grad/pallas_call | solution.py:115
  29.7 40.6 %all-to-all-done.1.own_ref = bf16[32,4,56,128]{3,2,1,0:T(8,128)(2,1)S(1)} async-done(((bf16[32,4,56,128]{3,2,1,0:T(8,128)(2,1)}), bf16[32,4,56,128]{3,2,1,0:T(8,128)(2,1)S(1)}, u32[]{:S(2)}, u32[]{:S(2)}) %all-to-all-start.1) | async-done | bytes 1835040 | tf_op jit(solution)/shard_map/all_to_all | solution.py:38
  70.3 1.3 copy-done
  71.6 6.9 %all-to-all-start.2 = ((bf16[32,4,48,128]{3,2,1,0:T(8,128)(2,1)}), bf16[32,4,48,128]{3,2,1,0:T(8,128)(2,1)S(1)}, u32[]{:S(2)}, u32[]{:S(2)}) async-start(bf16[32,4,48,128]{3,2,1,0:T(8,128)(2,1)} %pack_grad.1), calls=%async_computation.2 | async-start | bytes 3145728 | tf_op jit(solution)/shard_map/all_to_all | solution.py:38
  78.6 4.7 %split_features.1 = bf16[8,128,512]{2,1,0:T(8,128)(2,1)} custom-call(bf16[128,4096]{1,0:T(8,128)(2,1)} %bitcast.69), custom_call_target="tpu_custom_call" | custom-call | tf_op jit(solution)/shard_map/split_features/pallas_call | solution.py:144
  83.3 2.2 dynamic-slice_bitcast_fusion
  85.5 1.6 collective-permute-start.4
  87.1 2.9 %collective-permute-start.5 = (bf16[2,128,512]{2,1,0:T(8,128)(2,1)}, bf16[2,128,512]{2,1,0:T(8,128)(2,1)S(1)}, u32[]{:S(2)}, u32[]{:S(2)}) collective-permute-start(bf16[2,128,512]{2,1,0:T(8,128)(2,1)} %get-tuple-element.29), channel_id=1, source_target_pairs={{0,2},{1,3},{2,0},{3,1},{4,6},{5,7},{6,4},{7,5},{8,10},{9,11},{10,... | collective-permute-start | bytes 786440 | tf_op jit(solution)/shard_map/ppermute | solution.py:407
  90.0 3.0 %collective-permute-start.2 = (bf16[8,16,512]{2,1,0:T(8,128)(2,1)S(1)}, bf16[8,16,512]{2,1,0:T(8,128)(2,1)S(1)}, u32[]{:S(2)}, u32[]{:S(2)}) collective-permute-start(bf16[8,16,512]{2,1,0:T(8,128)(2,1)S(1)} %all-to-all-done), channel_id=1, source_target_pairs={{0,48},{16,0},{32,16},{48,32},{1,49},{17,1},{33,17},{49,33},{2,50}... | collective-permute-start | bytes 393224 | tf_op jit(solution)/shard_map/ppermute | solution.py:391
  93.0 0.9 collective-permute-start.1
  93.9 0.9 collective-permute-start
  94.7 6.0 %collective-permute-done.2 = bf16[8,16,512]{2,1,0:T(8,128)(2,1)S(1)} collective-permute-done((bf16[8,16,512]{2,1,0:T(8,128)(2,1)S(1)}, bf16[8,16,512]{2,1,0:T(8,128)(2,1)S(1)}, u32[]{:S(2)}, u32[]{:S(2)}) %collective-permute-start.2) | collective-permute-done | bytes 131104 | tf_op jit(solution)/shard_map/ppermute | solution.py:391
  100.8 1.2 collective-permute-start.6
  102.0 1.4 collective-permute-done.1
  103.4 1.1 collective-permute-done
  104.7 0.1 select_reduce_fusion.1
  104.8 0.6 pad_add_fusion.1.where_ref
  105.4 1.2 collective-permute-done.3.other_ref
  106.5 0.8 copy-done.15
  107.4 2.2 weight_rows.1
  109.7 0.7 copy-done.5
  110.5 2.9 %partial_values.1 = (bf16[128,512]{1,0:T(8,128)(2,1)}, bf16[128,512]{1,0:T(8,128)(2,1)}, bf16[128,512]{1,0:T(8,128)(2,1)}, bf16[128,512]{1,0:T(8,128)(2,1)}) custom-call(bf16[2,512,512]{2,1,0:T(8,128)(2,1)} %bitcast.60, bf16[2,128,512]{2,1,0:T(8,128)(2,1)} %get-tuple-element.31.refs_0_, bf16[2,128,512]{2,1,0:T(8,128)(2,1)} %copy-done.5, ...), custom_call_target="tpu_custom_call" | custom-call | tf_op jit(solution)/shard_map/partial_values/pallas_call | solution.py:188
  113.4 1.9 collective-permute-start.8
  115.3 1.3 collective-permute-start.7
  116.6 0.5 broadcast_add_fusion.doc_ref
  117.1 6.0 %collective-permute-done.9 = bf16[128,512]{1,0:T(8,128)(2,1)S(1)} collective-permute-done((bf16[128,512]{1,0:T(8,128)(2,1)}, bf16[128,512]{1,0:T(8,128)(2,1)S(1)}, u32[]{:S(2)}, u32[]{:S(2)}) %collective-permute-start.9) | collective-permute-done | bytes 131104 | tf_op jit(solution)/shard_map/ppermute | solution.py:412
  123.1 0.6 collective-permute-done.7
  123.8 1.9 fusion.1.v_ref
  125.6 6.8 %attend_probs.1 = (bf16[4,1536,256]{2,1,0:T(8,128)(2,1)}, bf16[4,256,1536]{2,1,0:T(8,128)(2,1)}) custom-call(s32[8]{0:T(128)} %broadcast_add_fusion.doc_ref, bf16[32,4,56,128]{3,2,1,0:T(8,128)(2,1)} %copy-done), custom_call_target="tpu_custom_call" | custom-call | tf_op jit(solution)/shard_map/attend_probs/pallas_call | solution.py:288
  132.4 1.2 copy-done.1
  133.6 4.6 %attend_value.1 = bf16[32,16,512]{2,1,0:T(8,128)(2,1)} custom-call(bf16[4,256,1536]{2,1,0:T(8,128)(2,1)} %get-tuple-element.20.p_ref, bf16[32,4,48,128]{3,2,1,0:T(8,128)(2,1)} %copy-done.1, bf16[32,8,512]{2,1,0:T(8,128)(2,1)} %fusion.1.v_ref), custom_call_target="tpu_custom_call" | custom-call | tf_op jit(solution)/shard_map/attend_value/pallas_call | solution.py:309
  138.2 25.7 %all_to_all.30.v_ref = bf16[32,16,512]{2,1,0:T(8,128)(2,1)S(1)} all-to-all(bf16[32,16,512]{2,1,0:T(8,128)(2,1)} %attend_value.1), channel_id=1, replica_groups=mesh['zh'=4,'x'=4,'core'=2,'zl'=2,'y'=4] {'zh','x','core'}, dimensions={0} | all-to-all | bytes 1048576 | tf_op jit(solution)/shard_map/all_to_all | solution.py:38
  163.9 0.2 convolution_convert_fusion.2.dv_ref
  164.2 1.1 broadcast_in_dim.25
  165.3 4.3 %all-to-all-start.4 = ((bf16[8,128,512]{2,1,0:T(8,128)(2,1)}), bf16[8,128,512]{2,1,0:T(8,128)(2,1)S(1)}, u32[]{:S(2)}, u32[]{:S(2)}) async-start(bf16[8,128,512]{2,1,0:T(8,128)(2,1)} %broadcast_in_dim.25), calls=%async_computation.4 | async-start | bytes 2097152 | tf_op jit(solution)/shard_map/all_to_all | solution.py:38
  169.6 0.9 dynamic-slice_bitcast_fusion.4
  170.7 2.1 collective-permute-start.10
  172.8 0.6 pad_add_fusion.2.source_ref
  173.4 21.7 %collective-permute-done.10.refs_4_ = bf16[4,128,512]{2,1,0:T(8,128)(2,1)S(1)} collective-permute-done((bf16[4,128,512]{2,1,0:T(8,128)(2,1)S(1)}, bf16[4,128,512]{2,1,0:T(8,128)(2,1)S(1)}, u32[]{:S(2)}, u32[]{:S(2)}) %collective-permute-start.10) | collective-permute-done | bytes 524320 | tf_op jit(solution)/shard_map/ppermute | solution.py:425
  195.1 0.8 copy-done.16
  195.9 2.4 token_rows_of.1
  198.3 8.9 %attend_query.1 = (bf16[6,32,4096]{2,1,0:T(8,128)(2,1)}, bf16[32,8,512]{2,1,0:T(8,128)(2,1)}) custom-call(bf16[4,1536,256]{2,1,0:T(8,128)(2,1)} %get-tuple-element.18.p_ref, bf16[32,4,56,128]{3,2,1,0:T(8,128)(2,1)} %copy-done, bf16[32,4,48,128]{3,2,1,0:T(8,128)(2,1)} %copy-done.1, bf16[32,16,512]{2,1,0:T(8,128)(2,1)} %copy-done.3), custom_call_target="tpu_custom_call" | custom-call | tf_op jit(solution)/shard_map/attend_query/pallas_call | solution.py:348
  207.2 0.7 fusion
  208.0 0.2 copy-done.17
  208.2 0.9 pad_maximum_fusion
  209.1 4.5 %all-to-all-start.5 = ((bf16[32,24,512]{2,1,0:T(8,128)(2,1)}), bf16[32,24,512]{2,1,0:T(8,128)(2,1)S(1)}, u32[]{:S(2)}, u32[]{:S(2)}) async-start(bf16[32,24,512]{2,1,0:T(8,128)(2,1)} %pad_maximum_fusion), calls=%async_computation.5 | async-start | bytes 1572864 | tf_op jit(solution)/shard_map/all_to_all | solution.py:38
  213.7 1.5 collective-permute-start.11
  215.2 2.8 %collective-permute-start.12 = (bf16[2,512,512]{2,1,0:T(8,128)(2,1)S(1)}, bf16[2,512,512]{2,1,0:T(8,128)(2,1)S(1)}, u32[]{:S(2)}, u32[]{:S(2)}) collective-permute-start(bf16[2,512,512]{2,1,0:T(8,128)(2,1)S(1)} %bitcast.63), channel_id=1, source_target_pairs={{0,2},{1,3},{2,0},{3,1},{4,6},{5,7},{6,4},{7,5},{8,10},{9,11},{10,... | collective-permute-start | bytes 3145736 | tf_op jit(solution)/shard_map/ppermute | solution.py:391
  218.0 1.4 collective-permute-start.13
  219.4 20.9 %collective-permute-done.11.refs_1_ = bf16[2,512,512]{2,1,0:T(8,128)(2,1)S(1)} collective-permute-done((bf16[2,512,512]{2,1,0:T(8,128)(2,1)S(1)}, bf16[2,512,512]{2,1,0:T(8,128)(2,1)S(1)}, u32[]{:S(2)}, u32[]{:S(2)}) %collective-permute-start.11) | collective-permute-done | bytes 1048608 | tf_op jit(solution)/shard_map/ppermute | solution.py:391
  240.3 23.4 %collective-permute-done.12.refs_2_ = bf16[2,512,512]{2,1,0:T(8,128)(2,1)S(1)} collective-permute-done((bf16[2,512,512]{2,1,0:T(8,128)(2,1)S(1)}, bf16[2,512,512]{2,1,0:T(8,128)(2,1)S(1)}, u32[]{:S(2)}, u32[]{:S(2)}) %collective-permute-start.12) | collective-permute-done | bytes 1048608 | tf_op jit(solution)/shard_map/ppermute | solution.py:391
  263.8 1.0 copy-done.14
  264.7 6.4 %make_input.1 = bf16[128,4096]{1,0:T(8,128)(2,1)} custom-call(s32[4]{0:T(128)} %copy-done.21, bf16[128,512]{1,0:T(8,128)(2,1)} %copy-done.11, bf16[2,512,512]{2,1,0:T(8,128)(2,1)} %bitcast.61, bf16[2,512,512]{2,1,0:T(8,128)(2,1)} %copy-done.13, bf16[2,512,512]{2,1,0:T(8,128)(2,1)} %copy-done.14, bf16[2,512,512]{2,1,0:T(8,128)(2,1)} %collective-permute-done.13.refs_3_), custom_call_target="tpu_custom_call" | custom-call | tf_op jit(solution)/shard_map/make_input/pallas_call | solution.py:215
  271.2 0.6 multiply_add_fusion
  271.8 0.9 fusion.2
  (60 shorter events, 0.8 us)
Async XLA Ops:
  2.0 15.9 %all-to-all-start = ((bf16[8,16,512]{2,1,0:T(8,128)(2,1)}), bf16[8,16,512]{2,1,0:T(8,128)(2,1)S(1)}, u32[]{:S(2)}, u32[]{:S(2)}) async-start(bf16[8,16,512]{2,1,0:T(8,128)(2,1)} %broadcast_in_dim.22), calls=%async_computation | async-start | bytes 262144 | tf_op jit(solution)/shard_map/all_to_all | solution.py:38
  17.9 52.5 %all-to-all-start.1 = ((bf16[32,4,56,128]{3,2,1,0:T(8,128)(2,1)}), bf16[32,4,56,128]{3,2,1,0:T(8,128)(2,1)S(1)}, u32[]{:S(2)}, u32[]{:S(2)}) async-start(bf16[32,4,56,128]{3,2,1,0:T(8,128)(2,1)} %pack_query.1), calls=%async_computation.1 | async-start | bytes 3670016 | tf_op jit(solution)/shard_map/all_to_all | solution.py:38
  70.3 1.3 copy-start
  71.6 60.8 %all-to-all-start.2 = ((bf16[32,4,48,128]{3,2,1,0:T(8,128)(2,1)}), bf16[32,4,48,128]{3,2,1,0:T(8,128)(2,1)S(1)}, u32[]{:S(2)}, u32[]{:S(2)}) async-start(bf16[32,4,48,128]{3,2,1,0:T(8,128)(2,1)} %pack_grad.1), calls=%async_computation.2 | async-start | bytes 3145728 | tf_op jit(solution)/shard_map/all_to_all | solution.py:38
  85.5 24.1 %collective-permute-start.4 = (bf16[2,128,512]{2,1,0:T(8,128)(2,1)}, bf16[2,128,512]{2,1,0:T(8,128)(2,1)S(1)}, u32[]{:S(2)}, u32[]{:S(2)}) collective-permute-start(bf16[2,128,512]{2,1,0:T(8,128)(2,1)} %get-tuple-element.30), channel_id=1, source_target_pairs={{0,1},{1,2},{2,3},{3,0},{4,5},{5,6},{6,7},{7,4},{8,9},{9,10},{10,1... | collective-permute-start | bytes 786440 | tf_op jit(solution)/shard_map/ppermute | solution.py:407
  87.1 22.5 %collective-permute-start.5 = (bf16[2,128,512]{2,1,0:T(8,128)(2,1)}, bf16[2,128,512]{2,1,0:T(8,128)(2,1)S(1)}, u32[]{:S(2)}, u32[]{:S(2)}) collective-permute-start(bf16[2,128,512]{2,1,0:T(8,128)(2,1)} %get-tuple-element.29), channel_id=1, source_target_pairs={{0,2},{1,3},{2,0},{3,1},{4,6},{5,7},{6,4},{7,5},{8,10},{9,11},{10,... | collective-permute-start | bytes 786440 | tf_op jit(solution)/shard_map/ppermute | solution.py:407
  90.0 10.8 %collective-permute-start.2 = (bf16[8,16,512]{2,1,0:T(8,128)(2,1)S(1)}, bf16[8,16,512]{2,1,0:T(8,128)(2,1)S(1)}, u32[]{:S(2)}, u32[]{:S(2)}) collective-permute-start(bf16[8,16,512]{2,1,0:T(8,128)(2,1)S(1)} %all-to-all-done), channel_id=1, source_target_pairs={{0,48},{16,0},{32,16},{48,32},{1,49},{17,1},{33,17},{49,33},{2,50}... | collective-permute-start | bytes 393224 | tf_op jit(solution)/shard_map/ppermute | solution.py:391
  93.0 10.4 %collective-permute-start.1 = (bf16[8,16,512]{2,1,0:T(8,128)(2,1)S(1)}, bf16[8,16,512]{2,1,0:T(8,128)(2,1)S(1)}, u32[]{:S(2)}, u32[]{:S(2)}) collective-permute-start(bf16[8,16,512]{2,1,0:T(8,128)(2,1)S(1)} %all-to-all-done), channel_id=1, source_target_pairs={{0,32},{16,48},{32,0},{48,16},{1,33},{17,49},{33,1},{49,17},{2,34}... | collective-permute-start | bytes 393224 | tf_op jit(solution)/shard_map/ppermute | solution.py:391
  93.9 10.6 %collective-permute-start = (bf16[8,16,512]{2,1,0:T(8,128)(2,1)S(1)}, bf16[8,16,512]{2,1,0:T(8,128)(2,1)S(1)}, u32[]{:S(2)}, u32[]{:S(2)}) collective-permute-start(bf16[8,16,512]{2,1,0:T(8,128)(2,1)S(1)} %all-to-all-done), channel_id=1, source_target_pairs={{0,16},{16,32},{32,48},{48,0},{1,17},{17,33},{33,49},{49,1},{2,18}... | collective-permute-start | bytes 393224 | tf_op jit(solution)/shard_map/ppermute | solution.py:391
  100.8 8.9 %collective-permute-start.6 = (bf16[2,128,512]{2,1,0:T(8,128)(2,1)}, bf16[2,128,512]{2,1,0:T(8,128)(2,1)S(1)}, u32[]{:S(2)}, u32[]{:S(2)}) collective-permute-start(bf16[2,128,512]{2,1,0:T(8,128)(2,1)} %get-tuple-element.28), channel_id=1, source_target_pairs={{0,3},{1,0},{2,1},{3,2},{4,7},{5,4},{6,5},{7,6},{8,11},{9,8},{10,9... | collective-permute-start | bytes 786440 | tf_op jit(solution)/shard_map/ppermute | solution.py:407
  104.5 2.0 copy-start.4
  104.5 2.0 collective-permute-start.3
  106.5 0.8 copy-start.15
  109.6 0.7 copy-start.5
  109.6 0.8 copy-start.7
  109.6 0.8 copy-start.9
  113.4 9.8 %collective-permute-start.9 = (bf16[128,512]{1,0:T(8,128)(2,1)}, bf16[128,512]{1,0:T(8,128)(2,1)S(1)}, u32[]{:S(2)}, u32[]{:S(2)}) collective-permute-start(bf16[128,512]{1,0:T(8,128)(2,1)} %get-tuple-element.25), channel_id=1, source_target_pairs={{0,1},{1,2},{2,3},{3,0},{4,5},{5,6},{6,7},{7,4},{8,9},{9,10},{10,1... | collective-permute-start | bytes 393224 | tf_op jit(solution)/shard_map/ppermute | solution.py:412
  113.4 9.8 %collective-permute-start.8 = (bf16[128,512]{1,0:T(8,128)(2,1)}, bf16[128,512]{1,0:T(8,128)(2,1)S(1)}, u32[]{:S(2)}, u32[]{:S(2)}) collective-permute-start(bf16[128,512]{1,0:T(8,128)(2,1)} %get-tuple-element.24), channel_id=1, source_target_pairs={{0,2},{1,3},{2,0},{3,1},{4,6},{5,7},{6,4},{7,5},{8,10},{9,11},{10,... | collective-permute-start | bytes 393224 | tf_op jit(solution)/shard_map/ppermute | solution.py:412
  115.3 8.4 %collective-permute-start.7 = (bf16[128,512]{1,0:T(8,128)(2,1)}, bf16[128,512]{1,0:T(8,128)(2,1)S(1)}, u32[]{:S(2)}, u32[]{:S(2)}) collective-permute-start(bf16[128,512]{1,0:T(8,128)(2,1)} %get-tuple-element.23), channel_id=1, source_target_pairs={{0,3},{1,0},{2,1},{3,2},{4,7},{5,4},{6,5},{7,6},{8,11},{9,8},{10,9... | collective-permute-start | bytes 393224 | tf_op jit(solution)/shard_map/ppermute | solution.py:412
  132.4 1.2 copy-start.1
  163.9 1.3 copy-start.3
  164.2 1.1 copy-start.11
  164.2 6.3 %copy-start.10 = (bf16[2,128,512]{2,1,0:T(8,128)(2,1)S(1)}, bf16[2,128,512]{2,1,0:T(8,128)(2,1)}, u32[]{:S(2)}) copy-start(bf16[2,128,512]{2,1,0:T(8,128)(2,1)} %copy-done.9) | copy-start | bytes 786436
  165.2 5.3 %copy-start.8 = (bf16[2,128,512]{2,1,0:T(8,128)(2,1)S(1)}, bf16[2,128,512]{2,1,0:T(8,128)(2,1)}, u32[]{:S(2)}) copy-start(bf16[2,128,512]{2,1,0:T(8,128)(2,1)} %copy-done.7) | copy-start | bytes 786436
  165.2 5.3 %copy-start.6 = (bf16[2,128,512]{2,1,0:T(8,128)(2,1)S(1)}, bf16[2,128,512]{2,1,0:T(8,128)(2,1)}, u32[]{:S(2)}) copy-start(bf16[2,128,512]{2,1,0:T(8,128)(2,1)} %copy-done.5) | copy-start | bytes 786436
  165.3 42.0 %all-to-all-start.4 = ((bf16[8,128,512]{2,1,0:T(8,128)(2,1)}), bf16[8,128,512]{2,1,0:T(8,128)(2,1)S(1)}, u32[]{:S(2)}, u32[]{:S(2)}) async-start(bf16[8,128,512]{2,1,0:T(8,128)(2,1)} %broadcast_in_dim.25), calls=%async_computation.4 | async-start | bytes 2097152 | tf_op jit(solution)/shard_map/all_to_all | solution.py:38
  170.7 24.4 %collective-permute-start.10 = (bf16[4,128,512]{2,1,0:T(8,128)(2,1)S(1)}, bf16[4,128,512]{2,1,0:T(8,128)(2,1)S(1)}, u32[]{:S(2)}, u32[]{:S(2)}) collective-permute-start(bf16[4,128,512]{2,1,0:T(8,128)(2,1)S(1)} %pad_maximum_fusion.2), channel_id=1, source_target_pairs={{0,4},{4,0},{1,5},{5,1},{2,6},{6,2},{3,7},{7,3},{8,12},{12,8},{9,1... | collective-permute-start | bytes 1572872 | tf_op jit(solution)/shard_map/ppermute | solution.py:425
  172.8 34.4 %copy-start.21 = (s32[4]{0:T(128)}, s32[4]{0:T(128)S(1)}, u32[]{:S(2)}) copy-start(s32[4]{0:T(128)S(1)} %and_select_fusion.peer_ref) | copy-start | bytes 52
  195.1 0.8 copy-start.16
  198.3 9.0 %copy-start.12 = (bf16[8,128,512]{2,1,0:T(8,128)(2,1)S(1)}, bf16[8,128,512]{2,1,0:T(8,128)(2,1)}, u32[]{:S(2)}) copy-start(bf16[8,128,512]{2,1,0:T(8,128)(2,1)} %token_rows_of.1) | copy-start | bytes 3145732
  207.2 1.0 copy-start.17
  208.2 5.5 %copy-start.2 = (bf16[2,32,16,512]{3,2,1,0:T(8,128)(2,1)S(1)}, bf16[2,32,16,512]{3,2,1,0:T(8,128)(2,1)}, u32[]{:S(2)}) copy-start(bf16[2,32,16,512]{3,2,1,0:T(8,128)(2,1)} %weight_rows.1) | copy-start | bytes 3145732
  209.1 62.0 %all-to-all-start.5 = ((bf16[32,24,512]{2,1,0:T(8,128)(2,1)}), bf16[32,24,512]{2,1,0:T(8,128)(2,1)S(1)}, u32[]{:S(2)}, u32[]{:S(2)}) async-start(bf16[32,24,512]{2,1,0:T(8,128)(2,1)} %pad_maximum_fusion), calls=%async_computation.5 | async-start | bytes 1572864 | tf_op jit(solution)/shard_map/all_to_all | solution.py:38
  213.6 57.5 %copy-start.18 = (bf16[16,512]{1,0:T(8,128)(2,1)S(1)}, bf16[16,512]{1,0:T(8,128)(2,1)}, u32[]{:S(2)}) copy-start(bf16[16,512]{1,0:T(8,128)(2,1)} %param.13) | copy-start | bytes 49156
  213.7 57.5 %copy-start.19 = (f32[16,512]{1,0:T(8,128)S(1)}, f32[16,512]{1,0:T(8,128)}, u32[]{:S(2)}) copy-start(f32[16,512]{1,0:T(8,128)} %param.15) | copy-start | bytes 98308
  213.7 57.5 %copy-start.20 = (f32[16,512]{1,0:T(8,128)S(1)}, f32[16,512]{1,0:T(8,128)}, u32[]{:S(2)}) copy-start(f32[16,512]{1,0:T(8,128)} %param.14) | copy-start | bytes 98308
  213.7 26.6 %collective-permute-start.11 = (bf16[2,512,512]{2,1,0:T(8,128)(2,1)S(1)}, bf16[2,512,512]{2,1,0:T(8,128)(2,1)S(1)}, u32[]{:S(2)}, u32[]{:S(2)}) collective-permute-start(bf16[2,512,512]{2,1,0:T(8,128)(2,1)S(1)} %bitcast.62), channel_id=1, source_target_pairs={{0,1},{1,2},{2,3},{3,0},{4,5},{5,6},{6,7},{7,4},{8,9},{9,10},{10,1... | collective-permute-start | bytes 3145736 | tf_op jit(solution)/shard_map/ppermute | solution.py:391
  215.2 48.6 %collective-permute-start.12 = (bf16[2,512,512]{2,1,0:T(8,128)(2,1)S(1)}, bf16[2,512,512]{2,1,0:T(8,128)(2,1)S(1)}, u32[]{:S(2)}, u32[]{:S(2)}) collective-permute-start(bf16[2,512,512]{2,1,0:T(8,128)(2,1)S(1)} %bitcast.63), channel_id=1, source_target_pairs={{0,2},{1,3},{2,0},{3,1},{4,6},{5,7},{6,4},{7,5},{8,10},{9,11},{10,... | collective-permute-start | bytes 3145736 | tf_op jit(solution)/shard_map/ppermute | solution.py:391
  218.0 46.7 %collective-permute-start.13 = (bf16[2,512,512]{2,1,0:T(8,128)(2,1)S(1)}, bf16[2,512,512]{2,1,0:T(8,128)(2,1)}, u32[]{:S(2)}, u32[]{:S(2)}) collective-permute-start(bf16[2,512,512]{2,1,0:T(8,128)(2,1)S(1)} %bitcast.64), channel_id=1, source_target_pairs={{0,3},{1,0},{2,1},{3,2},{4,7},{5,4},{6,5},{7,6},{8,11},{9,8},{10,9... | collective-permute-start | bytes 3145736 | tf_op jit(solution)/shard_map/ppermute | solution.py:391
  240.3 23.4 %copy-start.13 = (bf16[2,512,512]{2,1,0:T(8,128)(2,1)}, bf16[2,512,512]{2,1,0:T(8,128)(2,1)S(1)}, u32[]{:S(2)}) copy-start(bf16[2,512,512]{2,1,0:T(8,128)(2,1)S(1)} %collective-permute-done.11.refs_1_) | copy-start | bytes 3145732
  263.8 1.0 copy-start.14

commit v4 on v3

--- a/solution.py
+++ b/solution.py
@@ -160,9 +160,10 @@
     core = where_ref[4]
     for x in range(4):
         for z in range(8):
-            spot = (z // 2) * 8 + where_ref[x] * 2
-            out_ref[z % 2, spot + core] = same_ref[x, z]
-            out_ref[z % 2, spot + 1 - core] = other_ref[x, z]
+            place = where_ref[5 + z]
+            spot = (place >> 1) * 8 + where_ref[x] * 2
+            out_ref[place & 1, spot + core] = same_ref[x, z]
+            out_ref[place & 1, spot + 1 - core] = other_ref[x, z]
 
 
 def weight_rows(where, same, other):
@@ -383,7 +384,8 @@
 
     x, core, zl, y = (lax.axis_index(name) for name in ("x", "core", "zl", "y"))
     steps = jnp.arange(4, dtype=jnp.int32)
-    where = jnp.concatenate([(x - steps) % 4, core[None]])
+    zs = lax.axis_index(("zh", "zl"))
+    where = jnp.concatenate([(x - steps) % 4, core[None], (zs - jnp.arange(8, dtype=jnp.int32)) % 8])
     peers = (y - steps) % 4
 
     def around(value, axis):
@@ -392,10 +394,14 @@
             for k in (1, 2, 3)
         ]
 
-    column = exchange(jnp.broadcast_to(value_weight[None], (8,) + value_weight.shape), ("zh", "zl"))
+    ring = 8
+    column = [value_weight] + [
+        lax.ppermute(value_weight, ("zh", "zl"), [(i, (i + k) % ring) for i in range(ring)])
+        for k in range(1, ring)
+    ]
+    column = jnp.stack(column)
     query_split = pack_query(codes, query_rows, key_rows)
     token_split = split_features(token_rows)
-    query_split, column = lax.optimization_barrier((query_split, column))
     plane = jnp.stack(around(column, "x"))
     other = lax.ppermute(plane, "core", [(0, 1), (1, 0)])
     weight_part = weight_rows(where, plane, other).reshape(2, FEATS, -1)

time: 276 us -> 293 us (1.062)
  starting transfers between devices: 51.7 us -> 67.4 us
  waiting for transfers between devices: 125 us -> 121 us
  local copies, waits for them, and re-layouts: 11.7 us -> 15.1 us
    ppermute x0 -> x7, waiting for transfers between devices: none -> 20.8 us  [body(): lax.ppermute(value_weight, ('zh', 'zl'), [(i, (i + k) % ring) for i in ra...]
    ppermute x0 -> x7, starting transfers between devices: none -> 18.9 us  [body(): lax.ppermute(value_weight, ('zh', 'zl'), [(i, (i + k) % ring) for i in ra...]
    all_to_all x5 -> x4, waiting for transfers between devices: 43.1 us -> 24.7 us  [exchange(): return lax.all_to_all(value, axes, split_axis=0, concat_axis=0, tiled=True)]
    all_to_all x5 -> x4, starting transfers between devices: 30.2 us -> 23.2 us  [exchange(): return lax.all_to_all(value, axes, split_axis=0, concat_axis=0, tiled=True)]
    unnamed x44 -> x59, local copies, waits for them, and re-layouts: 6.14 us -> 10.9 us
    ppermute x6, waiting for transfers between devices: 52.9 us -> 48.2 us  [around(): lax.ppermute(value, axis, [(i, (i + k) % 4) for i in range(4)])]
  transfers between devices with their start and end apart: 19 -> 25, of which waited for: 11 -> 10; matrix products, arithmetic and copies ran while one was open for 3% -> 4% of each run, Pallas kernels for 16% -> 13%
where the time goes in v4:
time: 293 us; the launch traced here: 289 us
  waiting for transfers between devices  121 us (41%)
  starting transfers between devices  67.4 us (23%)
  Pallas kernels  47.6 us (16%)
  blocking collectives  25.5 us (9%)
  local copies, waits for them, and re-layouts  15.1 us (5%)
  other arithmetic  7.84 us (3%)
  matrix products  3.72 us (1%)
    ppermute x6, waiting for transfers between devices, around(): lax.ppermute(value, axis, [(i, (i + k) % 4) for i in range(4)])  48.2 us
    all_to_all x1, blocking collectives, exchange(): return lax.all_to_all(value, axes, split_axis=0, concat_axis=0, tiled=True)  25.5 us
    all_to_all x4, waiting for transfers between devices, exchange(): return lax.all_to_all(value, axes, split_axis=0, concat_axis=0, tiled=True)  24.7 us
    all_to_all x4, starting transfers between devices, exchange(): return lax.all_to_all(value, axes, split_axis=0, concat_axis=0, tiled=True)  23.2 us
    ppermute x1, waiting for transfers between devices, body(): crossed = lax.ppermute(crossed, 'zl', [(0, 1), (1, 0)])  22.5 us
    ppermute x7, waiting for transfers between devices, body(): lax.ppermute(value_weight, ('zh', 'zl'), [(i, (i + k) % ring) for i in ra...  20.8 us
    ppermute x7, starting transfers between devices, body(): lax.ppermute(value_weight, ('zh', 'zl'), [(i, (i + k) % ring) for i in ra...  18.9 us
    unnamed x59, local copies, waits for them, and re-layouts  10.9 us
  transfers between devices with their start and end apart: 25, of which 10 were waited for; matrix products, arithmetic and copies ran while one was open for 4% of the time, Pallas kernels for 13%

profile of v4, /device:TPU:0, one launch (start us, length us, event | category | flops | bytes accessed | tf_op | source)
XLA Modules:
  0.0 289.5 jit_solution(18306887559326821353)
XLA Ops:
  0.6 0.7 fusion.12
  1.9 0.7 select_reduce_fusion
  4.0 4.4 %pack_query.1 = bf16[32,4,56,128]{3,2,1,0:T(8,128)(2,1)} custom-call(s32[2,128]{1,0:T(2,128)} %pad_add_fusion.code_ref, bf16[128,4096]{1,0:T(8,128)(2,1)} %bitcast.84, bf16[128,512]{1,0:T(8,128)(2,1)} %bitcast.89), custom_call_target="tpu_custom_call" | custom-call | tf_op jit(solution)/shard_map/pack_query/pallas_call | solution.py:99
  8.4 9.7 %all-to-all-start = ((bf16[32,4,56,128]{3,2,1,0:T(8,128)(2,1)}), bf16[32,4,56,128]{3,2,1,0:T(8,128)(2,1)S(1)}, u32[]{:S(2)}, u32[]{:S(2)}) async-start(bf16[32,4,56,128]{3,2,1,0:T(8,128)(2,1)} %pack_query.1), calls=%async_computation | async-start | bytes 3670016 | tf_op jit(solution)/shard_map/all_to_all | solution.py:38
  18.2 1.1 collective-permute-start
  19.3 2.7 collective-permute-start.1
  22.0 3.2 %collective-permute-start.2 = (bf16[16,512]{1,0:T(8,128)(2,1)S(1)}, bf16[16,512]{1,0:T(8,128)(2,1)}, u32[]{:S(2)}, u32[]{:S(2)}) collective-permute-start(bf16[16,512]{1,0:T(8,128)(2,1)S(1)} %copy-done.18), channel_id=1, source_target_pairs={{0,68},{4,128},{64,132},{68,192},{128,196},{132,0},{192,4},{196,64... | collective-permute-start | bytes 49160 | tf_op jit(solution)/shard_map/ppermute | solution.py:399
  25.1 2.3 collective-permute-start.3
  27.4 3.2 %collective-permute-start.4 = (bf16[16,512]{1,0:T(8,128)(2,1)S(1)}, bf16[16,512]{1,0:T(8,128)(2,1)}, u32[]{:S(2)}, u32[]{:S(2)}) collective-permute-start(bf16[16,512]{1,0:T(8,128)(2,1)S(1)} %copy-done.18), channel_id=1, source_target_pairs={{0,132},{4,192},{64,196},{68,0},{128,4},{132,64},{192,68},{196,128... | collective-permute-start | bytes 49160 | tf_op jit(solution)/shard_map/ppermute | solution.py:399
  30.6 4.2 %pack_grad.1 = bf16[32,4,48,128]{3,2,1,0:T(8,128)(2,1)} custom-call(s32[2,128]{1,0:T(2,128)} %pad_add_fusion.code_ref, bf16[128,4096]{1,0:T(8,128)(2,1)} %bitcast.83), custom_call_target="tpu_custom_call" | custom-call | tf_op jit(solution)/shard_map/pack_grad/pallas_call | solution.py:115
  34.8 4.7 %split_features.1 = bf16[8,128,512]{2,1,0:T(8,128)(2,1)} custom-call(bf16[128,4096]{1,0:T(8,128)(2,1)} %bitcast.85), custom_call_target="tpu_custom_call" | custom-call | tf_op jit(solution)/shard_map/split_features/pallas_call | solution.py:144
  39.5 24.7 %all-to-all-done.own_ref = bf16[32,4,56,128]{3,2,1,0:T(8,128)(2,1)S(1)} async-done(((bf16[32,4,56,128]{3,2,1,0:T(8,128)(2,1)}), bf16[32,4,56,128]{3,2,1,0:T(8,128)(2,1)S(1)}, u32[]{:S(2)}, u32[]{:S(2)}) %all-to-all-start) | async-done | bytes 1835040 | tf_op jit(solution)/shard_map/all_to_all | solution.py:38
  64.3 1.3 copy-done
  65.6 5.4 %all-to-all-start.1 = ((bf16[32,4,48,128]{3,2,1,0:T(8,128)(2,1)}), bf16[32,4,48,128]{3,2,1,0:T(8,128)(2,1)S(1)}, u32[]{:S(2)}, u32[]{:S(2)}) async-start(bf16[32,4,48,128]{3,2,1,0:T(8,128)(2,1)} %pack_grad.1), calls=%async_computation.1 | async-start | bytes 3145728 | tf_op jit(solution)/shard_map/all_to_all | solution.py:38
  71.0 2.2 dynamic-slice_bitcast_fusion
  73.2 3.9 %collective-permute-start.5 = (bf16[16,512]{1,0:T(8,128)(2,1)S(1)}, bf16[16,512]{1,0:T(8,128)(2,1)S(1)}, u32[]{:S(2)}, u32[]{:S(2)}) collective-permute-start(bf16[16,512]{1,0:T(8,128)(2,1)S(1)} %copy-done.18), channel_id=1, source_target_pairs={{0,192},{4,196},{64,0},{68,4},{128,64},{132,68},{192,128},{196,132... | collective-permute-start | bytes 49160 | tf_op jit(solution)/shard_map/ppermute | solution.py:399
  77.2 0.7 constant_dynamic-update-slice_fusion.6
  77.9 2.5 collective-permute-start.6
  80.4 0.7 constant_dynamic-update-slice_fusion.5
  81.1 1.6 collective-permute-start.11
  82.7 0.7 constant_dynamic-update-slice_fusion.4
  83.4 2.9 %collective-permute-start.12 = (bf16[2,128,512]{2,1,0:T(8,128)(2,1)}, bf16[2,128,512]{2,1,0:T(8,128)(2,1)S(1)}, u32[]{:S(2)}, u32[]{:S(2)}) collective-permute-start(bf16[2,128,512]{2,1,0:T(8,128)(2,1)} %get-tuple-element.25), channel_id=1, source_target_pairs={{0,2},{1,3},{2,0},{3,1},{4,6},{5,7},{6,4},{7,5},{8,10},{9,11},{10,... | collective-permute-start | bytes 786440 | tf_op jit(solution)/shard_map/ppermute | solution.py:413
  86.3 0.7 constant_dynamic-update-slice_fusion.3
  87.0 0.7 constant_dynamic-update-slice_fusion.2
  87.8 7.2 %collective-permute-done.5 = bf16[16,512]{1,0:T(8,128)(2,1)S(1)} collective-permute-done((bf16[16,512]{1,0:T(8,128)(2,1)S(1)}, bf16[16,512]{1,0:T(8,128)(2,1)S(1)}, u32[]{:S(2)}, u32[]{:S(2)}) %collective-permute-start.5) | collective-permute-done | bytes 16416 | tf_op jit(solution)/shard_map/ppermute | solution.py:399
  95.0 13.6 %collective-permute-done.6 = bf16[16,512]{1,0:T(8,128)(2,1)S(1)} collective-permute-done((bf16[16,512]{1,0:T(8,128)(2,1)S(1)}, bf16[16,512]{1,0:T(8,128)(2,1)S(1)}, u32[]{:S(2)}, u32[]{:S(2)}) %collective-permute-start.6) | collective-permute-done | bytes 16416 | tf_op jit(solution)/shard_map/ppermute | solution.py:399
  108.6 2.7 collective-permute-start.9
  111.3 1.0 collective-permute-start.8
  113.3 3.0 %collective-permute-done.9 = bf16[8,16,512]{2,1,0:T(8,128)(2,1)S(1)} collective-permute-done((bf16[8,16,512]{2,1,0:T(8,128)(2,1)S(1)}, bf16[8,16,512]{2,1,0:T(8,128)(2,1)S(1)}, u32[]{:S(2)}, u32[]{:S(2)}) %collective-permute-start.9) | collective-permute-done | bytes 131104 | tf_op jit(solution)/shard_map/ppermute | solution.py:393
  116.3 3.0 %collective-permute-start.13 = (bf16[2,128,512]{2,1,0:T(8,128)(2,1)}, bf16[2,128,512]{2,1,0:T(8,128)(2,1)S(1)}, u32[]{:S(2)}, u32[]{:S(2)}) collective-permute-start(bf16[2,128,512]{2,1,0:T(8,128)(2,1)} %get-tuple-element.24), channel_id=1, source_target_pairs={{0,3},{1,0},{2,1},{3,2},{4,7},{5,4},{6,5},{7,6},{8,11},{9,8},{10,9... | collective-permute-start | bytes 786440 | tf_op jit(solution)/shard_map/ppermute | solution.py:413
  120.2 0.8 select_reduce_fusion.1
  121.6 0.7 multiply_add_fusion.1
  122.3 0.8 copy-done.15
  123.1 2.3 weight_rows.1
  126.3 2.9 partial_values.1
  129.2 1.6 collective-permute-start.16
  130.8 2.9 %collective-permute-start.15 = (bf16[128,512]{1,0:T(8,128)(2,1)}, bf16[128,512]{1,0:T(8,128)(2,1)S(1)}, u32[]{:S(2)}, u32[]{:S(2)}) collective-permute-start(bf16[128,512]{1,0:T(8,128)(2,1)} %get-tuple-element.20), channel_id=1, source_target_pairs={{0,2},{1,3},{2,0},{3,1},{4,6},{5,7},{6,4},{7,5},{8,10},{9,11},{10,... | collective-permute-start | bytes 393224 | tf_op jit(solution)/shard_map/ppermute | solution.py:418
  133.7 1.3 collective-permute-start.14
  135.5 1.0 collective-permute-done.16
  136.5 4.0 %collective-permute-done.15 = bf16[128,512]{1,0:T(8,128)(2,1)S(1)} collective-permute-done((bf16[128,512]{1,0:T(8,128)(2,1)}, bf16[128,512]{1,0:T(8,128)(2,1)S(1)}, u32[]{:S(2)}, u32[]{:S(2)}) %collective-permute-start.15) | collective-permute-done | bytes 131104 | tf_op jit(solution)/shard_map/ppermute | solution.py:418
  140.5 1.9 fusion.1.v_ref
  142.4 6.7 %attend_probs.1 = (bf16[4,1536,256]{2,1,0:T(8,128)(2,1)}, bf16[4,256,1536]{2,1,0:T(8,128)(2,1)}) custom-call(s32[8]{0:T(128)} %broadcast_add_fusion.doc_ref, bf16[32,4,56,128]{3,2,1,0:T(8,128)(2,1)} %copy-done), custom_call_target="tpu_custom_call" | custom-call | tf_op jit(solution)/shard_map/attend_probs/pallas_call | solution.py:289
  149.1 1.2 copy-done.1
  150.3 4.6 %attend_value.1 = bf16[32,16,512]{2,1,0:T(8,128)(2,1)} custom-call(bf16[4,256,1536]{2,1,0:T(8,128)(2,1)} %get-tuple-element.17.p_ref, bf16[32,4,48,128]{3,2,1,0:T(8,128)(2,1)} %copy-done.1, bf16[32,8,512]{2,1,0:T(8,128)(2,1)} %fusion.1.v_ref), custom_call_target="tpu_custom_call" | custom-call | tf_op jit(solution)/shard_map/attend_value/pallas_call | solution.py:310
  154.9 25.5 %all_to_all.25.v_ref = bf16[32,16,512]{2,1,0:T(8,128)(2,1)S(1)} all-to-all(bf16[32,16,512]{2,1,0:T(8,128)(2,1)} %attend_value.1), channel_id=1, replica_groups=mesh['zh'=4,'x'=4,'core'=2,'zl'=2,'y'=4] {'zh','x','core'}, dimensions={0} | all-to-all | bytes 1048576 | tf_op jit(solution)/shard_map/all_to_all | solution.py:38
  180.6 1.1 broadcast_in_dim.22
  181.7 3.7 %all-to-all-start.3 = ((bf16[8,128,512]{2,1,0:T(8,128)(2,1)}), bf16[8,128,512]{2,1,0:T(8,128)(2,1)S(1)}, u32[]{:S(2)}, u32[]{:S(2)}) async-start(bf16[8,128,512]{2,1,0:T(8,128)(2,1)} %broadcast_in_dim.22), calls=%async_computation.3 | async-start | bytes 2097152 | tf_op jit(solution)/shard_map/all_to_all | solution.py:38
  185.4 0.9 dynamic-slice_bitcast_fusion.4
  186.5 2.1 collective-permute-start.17
  189.3 22.5 %collective-permute-done.17.refs_4_ = bf16[4,128,512]{2,1,0:T(8,128)(2,1)S(1)} collective-permute-done((bf16[4,128,512]{2,1,0:T(8,128)(2,1)S(1)}, bf16[4,128,512]{2,1,0:T(8,128)(2,1)S(1)}, u32[]{:S(2)}, u32[]{:S(2)}) %collective-permute-start.17) | collective-permute-done | bytes 524320 | tf_op jit(solution)/shard_map/ppermute | solution.py:431
  211.8 0.8 copy-done.16
  212.6 2.4 token_rows_of.1
  215.0 8.9 %attend_query.1 = (bf16[6,32,4096]{2,1,0:T(8,128)(2,1)}, bf16[32,8,512]{2,1,0:T(8,128)(2,1)}) custom-call(bf16[4,1536,256]{2,1,0:T(8,128)(2,1)} %get-tuple-element.15.p_ref, bf16[32,4,56,128]{3,2,1,0:T(8,128)(2,1)} %copy-done, bf16[32,4,48,128]{3,2,1,0:T(8,128)(2,1)} %copy-done.1, bf16[32,16,512]{2,1,0:T(8,128)(2,1)} %copy-done.3), custom_call_target="tpu_custom_call" | custom-call | tf_op jit(solution)/shard_map/attend_query/pallas_call | solution.py:349
  223.9 0.7 fusion
  224.9 0.9 pad_maximum_fusion
  225.8 4.3 %all-to-all-start.4 = ((bf16[32,24,512]{2,1,0:T(8,128)(2,1)}), bf16[32,24,512]{2,1,0:T(8,128)(2,1)S(1)}, u32[]{:S(2)}, u32[]{:S(2)}) async-start(bf16[32,24,512]{2,1,0:T(8,128)(2,1)} %pad_maximum_fusion), calls=%async_computation.4 | async-start | bytes 1572864 | tf_op jit(solution)/shard_map/all_to_all | solution.py:38
  230.2 1.5 collective-permute-start.18
  231.7 3.0 %collective-permute-start.19 = (bf16[2,512,512]{2,1,0:T(8,128)(2,1)S(1)}, bf16[2,512,512]{2,1,0:T(8,128)(2,1)S(1)}, u32[]{:S(2)}, u32[]{:S(2)}) collective-permute-start(bf16[2,512,512]{2,1,0:T(8,128)(2,1)S(1)} %bitcast.79), channel_id=1, source_target_pairs={{0,2},{1,3},{2,0},{3,1},{4,6},{5,7},{6,4},{7,5},{8,10},{9,11},{10,... | collective-permute-start | bytes 3145736 | tf_op jit(solution)/shard_map/ppermute | solution.py:393
  234.7 1.2 collective-permute-start.20
  235.8 21.0 %collective-permute-done.18.refs_1_ = bf16[2,512,512]{2,1,0:T(8,128)(2,1)S(1)} collective-permute-done((bf16[2,512,512]{2,1,0:T(8,128)(2,1)S(1)}, bf16[2,512,512]{2,1,0:T(8,128)(2,1)S(1)}, u32[]{:S(2)}, u32[]{:S(2)}) %collective-permute-start.18) | collective-permute-done | bytes 1048608 | tf_op jit(solution)/shard_map/ppermute | solution.py:393
  256.8 23.6 %collective-permute-done.19.refs_2_ = bf16[2,512,512]{2,1,0:T(8,128)(2,1)S(1)} collective-permute-done((bf16[2,512,512]{2,1,0:T(8,128)(2,1)S(1)}, bf16[2,512,512]{2,1,0:T(8,128)(2,1)S(1)}, u32[]{:S(2)}, u32[]{:S(2)}) %collective-permute-start.19) | collective-permute-done | bytes 1048608 | tf_op jit(solution)/shard_map/ppermute | solution.py:393
  280.5 1.0 copy-done.14
  281.4 6.4 %make_input.1 = bf16[128,4096]{1,0:T(8,128)(2,1)} custom-call(s32[4]{0:T(128)} %copy-done.22, bf16[128,512]{1,0:T(8,128)(2,1)} %copy-done.11, bf16[2,512,512]{2,1,0:T(8,128)(2,1)} %bitcast.77, bf16[2,512,512]{2,1,0:T(8,128)(2,1)} %copy-done.13, bf16[2,512,512]{2,1,0:T(8,128)(2,1)} %copy-done.14, bf16[2,512,512]{2,1,0:T(8,128)(2,1)} %collective-permute-done.20.refs_3_), custom_call_target="tpu_custom_call" | custom-call | tf_op jit(solution)/shard_map/make_input/pallas_call | solution.py:216
  288.6 0.9 fusion.2
  (88 shorter events, 7.7 us)
Async XLA Ops:
  1.4 0.5 copy-start.25
  2.6 1.4 copy-start.23
  2.8 0.6 copy-start.21
  8.4 9.8 %copy-start.18 = (bf16[16,512]{1,0:T(8,128)(2,1)S(1)}, bf16[16,512]{1,0:T(8,128)(2,1)}, u32[]{:S(2)}) copy-start(bf16[16,512]{1,0:T(8,128)(2,1)} %param.13) | copy-start | bytes 49156
  8.4 55.8 %all-to-all-start = ((bf16[32,4,56,128]{3,2,1,0:T(8,128)(2,1)}), bf16[32,4,56,128]{3,2,1,0:T(8,128)(2,1)S(1)}, u32[]{:S(2)}, u32[]{:S(2)}) async-start(bf16[32,4,56,128]{3,2,1,0:T(8,128)(2,1)} %pack_query.1), calls=%async_computation | async-start | bytes 3670016 | tf_op jit(solution)/shard_map/all_to_all | solution.py:38
  18.2 55.0 %collective-permute-start = (bf16[16,512]{1,0:T(8,128)(2,1)S(1)}, bf16[16,512]{1,0:T(8,128)(2,1)}, u32[]{:S(2)}, u32[]{:S(2)}) collective-permute-start(bf16[16,512]{1,0:T(8,128)(2,1)S(1)} %copy-done.18), channel_id=1, source_target_pairs={{0,4},{4,64},{64,68},{68,128},{128,132},{132,192},{192,196},{196,0... | collective-permute-start | bytes 49160 | tf_op jit(solution)/shard_map/ppermute | solution.py:399
  19.3 58.6 %collective-permute-start.1 = (bf16[16,512]{1,0:T(8,128)(2,1)S(1)}, bf16[16,512]{1,0:T(8,128)(2,1)}, u32[]{:S(2)}, u32[]{:S(2)}) collective-permute-start(bf16[16,512]{1,0:T(8,128)(2,1)S(1)} %copy-done.18), channel_id=1, source_target_pairs={{0,64},{4,68},{64,128},{68,132},{128,192},{132,196},{192,0},{196,4... | collective-permute-start | bytes 49160 | tf_op jit(solution)/shard_map/ppermute | solution.py:399
  22.0 59.1 %collective-permute-start.2 = (bf16[16,512]{1,0:T(8,128)(2,1)S(1)}, bf16[16,512]{1,0:T(8,128)(2,1)}, u32[]{:S(2)}, u32[]{:S(2)}) collective-permute-start(bf16[16,512]{1,0:T(8,128)(2,1)S(1)} %copy-done.18), channel_id=1, source_target_pairs={{0,68},{4,128},{64,132},{68,192},{128,196},{132,0},{192,4},{196,64... | collective-permute-start | bytes 49160 | tf_op jit(solution)/shard_map/ppermute | solution.py:399
  25.1 58.3 %collective-permute-start.3 = (bf16[16,512]{1,0:T(8,128)(2,1)S(1)}, bf16[16,512]{1,0:T(8,128)(2,1)}, u32[]{:S(2)}, u32[]{:S(2)}) collective-permute-start(bf16[16,512]{1,0:T(8,128)(2,1)S(1)} %copy-done.18), channel_id=1, source_target_pairs={{0,128},{4,132},{64,192},{68,196},{128,0},{132,4},{192,64},{196,68... | collective-permute-start | bytes 49160 | tf_op jit(solution)/shard_map/ppermute | solution.py:399
  27.4 59.6 %collective-permute-start.4 = (bf16[16,512]{1,0:T(8,128)(2,1)S(1)}, bf16[16,512]{1,0:T(8,128)(2,1)}, u32[]{:S(2)}, u32[]{:S(2)}) collective-permute-start(bf16[16,512]{1,0:T(8,128)(2,1)S(1)} %copy-done.18), channel_id=1, source_target_pairs={{0,132},{4,192},{64,196},{68,0},{128,4},{132,64},{192,68},{196,128... | collective-permute-start | bytes 49160 | tf_op jit(solution)/shard_map/ppermute | solution.py:399
  64.3 1.3 copy-start
  65.6 83.5 %all-to-all-start.1 = ((bf16[32,4,48,128]{3,2,1,0:T(8,128)(2,1)}), bf16[32,4,48,128]{3,2,1,0:T(8,128)(2,1)S(1)}, u32[]{:S(2)}, u32[]{:S(2)}) async-start(bf16[32,4,48,128]{3,2,1,0:T(8,128)(2,1)} %pack_grad.1), calls=%async_computation.1 | async-start | bytes 3145728 | tf_op jit(solution)/shard_map/all_to_all | solution.py:38
  71.0 41.8 %copy-start.24 = (s32[128]{0:T(128)S(1)}, s32[128]{0:T(128)}, u32[]{:S(2)}) copy-start(s32[128]{0:T(128)} %copy-done.23) | copy-start | bytes 1540
  73.2 21.8 %collective-permute-start.5 = (bf16[16,512]{1,0:T(8,128)(2,1)S(1)}, bf16[16,512]{1,0:T(8,128)(2,1)S(1)}, u32[]{:S(2)}, u32[]{:S(2)}) collective-permute-start(bf16[16,512]{1,0:T(8,128)(2,1)S(1)} %copy-done.18), channel_id=1, source_target_pairs={{0,192},{4,196},{64,0},{68,4},{128,64},{132,68},{192,128},{196,132... | collective-permute-start | bytes 49160 | tf_op jit(solution)/shard_map/ppermute | solution.py:399
  77.9 30.7 %collective-permute-start.6 = (bf16[16,512]{1,0:T(8,128)(2,1)S(1)}, bf16[16,512]{1,0:T(8,128)(2,1)S(1)}, u32[]{:S(2)}, u32[]{:S(2)}) collective-permute-start(bf16[16,512]{1,0:T(8,128)(2,1)S(1)} %copy-done.18), channel_id=1, source_target_pairs={{0,196},{4,0},{64,4},{68,64},{128,68},{132,128},{192,132},{196,192... | collective-permute-start | bytes 49160 | tf_op jit(solution)/shard_map/ppermute | solution.py:399
  81.1 44.3 %collective-permute-start.11 = (bf16[2,128,512]{2,1,0:T(8,128)(2,1)}, bf16[2,128,512]{2,1,0:T(8,128)(2,1)S(1)}, u32[]{:S(2)}, u32[]{:S(2)}) collective-permute-start(bf16[2,128,512]{2,1,0:T(8,128)(2,1)} %get-tuple-element.26), channel_id=1, source_target_pairs={{0,1},{1,2},{2,3},{3,0},{4,5},{5,6},{6,7},{7,4},{8,9},{9,10},{10,1... | collective-permute-start | bytes 786440 | tf_op jit(solution)/shard_map/ppermute | solution.py:413
  83.4 42.0 %collective-permute-start.12 = (bf16[2,128,512]{2,1,0:T(8,128)(2,1)}, bf16[2,128,512]{2,1,0:T(8,128)(2,1)S(1)}, u32[]{:S(2)}, u32[]{:S(2)}) collective-permute-start(bf16[2,128,512]{2,1,0:T(8,128)(2,1)} %get-tuple-element.25), channel_id=1, source_target_pairs={{0,2},{1,3},{2,0},{3,1},{4,6},{5,7},{6,4},{7,5},{8,10},{9,11},{10,... | collective-permute-start | bytes 786440 | tf_op jit(solution)/shard_map/ppermute | solution.py:413
  108.6 7.7 %collective-permute-start.9 = (bf16[8,16,512]{2,1,0:T(8,128)(2,1)S(1)}, bf16[8,16,512]{2,1,0:T(8,128)(2,1)S(1)}, u32[]{:S(2)}, u32[]{:S(2)}) collective-permute-start(bf16[8,16,512]{2,1,0:T(8,128)(2,1)S(1)} %constant_dynamic-update-slice_fusion), channel_id=1, source_target_pairs={{0,48},{16,0},{32,16},{48,32},{1,49},{17,1},{33,17},{49,33},{2,50}... | collective-permute-start | bytes 393224 | tf_op jit(solution)/shard_map/ppermute | solution.py:393
  111.3 8.0 %collective-permute-start.8 = (bf16[8,16,512]{2,1,0:T(8,128)(2,1)S(1)}, bf16[8,16,512]{2,1,0:T(8,128)(2,1)S(1)}, u32[]{:S(2)}, u32[]{:S(2)}) collective-permute-start(bf16[8,16,512]{2,1,0:T(8,128)(2,1)S(1)} %constant_dynamic-update-slice_fusion), channel_id=1, source_target_pairs={{0,32},{16,48},{32,0},{48,16},{1,33},{17,49},{33,1},{49,17},{2,34}... | collective-permute-start | bytes 393224 | tf_op jit(solution)/shard_map/ppermute | solution.py:393
  112.3 7.7 %collective-permute-start.7 = (bf16[8,16,512]{2,1,0:T(8,128)(2,1)S(1)}, bf16[8,16,512]{2,1,0:T(8,128)(2,1)S(1)}, u32[]{:S(2)}, u32[]{:S(2)}) collective-permute-start(bf16[8,16,512]{2,1,0:T(8,128)(2,1)S(1)} %constant_dynamic-update-slice_fusion), channel_id=1, source_target_pairs={{0,16},{16,32},{32,48},{48,0},{1,17},{17,33},{33,49},{49,1},{2,18}... | collective-permute-start | bytes 393224 | tf_op jit(solution)/shard_map/ppermute | solution.py:393
  116.3 9.1 %collective-permute-start.13 = (bf16[2,128,512]{2,1,0:T(8,128)(2,1)}, bf16[2,128,512]{2,1,0:T(8,128)(2,1)S(1)}, u32[]{:S(2)}, u32[]{:S(2)}) collective-permute-start(bf16[2,128,512]{2,1,0:T(8,128)(2,1)} %get-tuple-element.24), channel_id=1, source_target_pairs={{0,3},{1,0},{2,1},{3,2},{4,7},{5,4},{6,5},{7,6},{8,11},{9,8},{10,9... | collective-permute-start | bytes 786440 | tf_op jit(solution)/shard_map/ppermute | solution.py:413
  120.0 2.2 copy-start.4
  120.1 2.2 collective-permute-start.10
  122.3 0.8 copy-start.15
  125.4 0.7 copy-start.5
  125.4 0.8 copy-start.7
  125.4 0.9 copy-start.9
  129.2 7.3 %collective-permute-start.16 = (bf16[128,512]{1,0:T(8,128)(2,1)}, bf16[128,512]{1,0:T(8,128)(2,1)S(1)}, u32[]{:S(2)}, u32[]{:S(2)}) collective-permute-start(bf16[128,512]{1,0:T(8,128)(2,1)} %get-tuple-element.21), channel_id=1, source_target_pairs={{0,1},{1,2},{2,3},{3,0},{4,5},{5,6},{6,7},{7,4},{8,9},{9,10},{10,1... | collective-permute-start | bytes 393224 | tf_op jit(solution)/shard_map/ppermute | solution.py:418
  130.8 9.7 %collective-permute-start.15 = (bf16[128,512]{1,0:T(8,128)(2,1)}, bf16[128,512]{1,0:T(8,128)(2,1)S(1)}, u32[]{:S(2)}, u32[]{:S(2)}) collective-permute-start(bf16[128,512]{1,0:T(8,128)(2,1)} %get-tuple-element.20), channel_id=1, source_target_pairs={{0,2},{1,3},{2,0},{3,1},{4,6},{5,7},{6,4},{7,5},{8,10},{9,11},{10,... | collective-permute-start | bytes 393224 | tf_op jit(solution)/shard_map/ppermute | solution.py:418
  133.7 6.8 %collective-permute-start.14 = (bf16[128,512]{1,0:T(8,128)(2,1)}, bf16[128,512]{1,0:T(8,128)(2,1)S(1)}, u32[]{:S(2)}, u32[]{:S(2)}) collective-permute-start(bf16[128,512]{1,0:T(8,128)(2,1)} %get-tuple-element.19), channel_id=1, source_target_pairs={{0,3},{1,0},{2,1},{3,2},{4,7},{5,4},{6,5},{7,6},{8,11},{9,8},{10,9... | collective-permute-start | bytes 393224 | tf_op jit(solution)/shard_map/ppermute | solution.py:418
  149.1 1.2 copy-start.1
  180.4 1.3 copy-start.3
  180.6 1.1 copy-start.11
  180.6 5.8 %copy-start.10 = (bf16[2,128,512]{2,1,0:T(8,128)(2,1)S(1)}, bf16[2,128,512]{2,1,0:T(8,128)(2,1)}, u32[]{:S(2)}) copy-start(bf16[2,128,512]{2,1,0:T(8,128)(2,1)} %copy-done.9) | copy-start | bytes 786436
  181.7 4.7 %copy-start.8 = (bf16[2,128,512]{2,1,0:T(8,128)(2,1)S(1)}, bf16[2,128,512]{2,1,0:T(8,128)(2,1)}, u32[]{:S(2)}) copy-start(bf16[2,128,512]{2,1,0:T(8,128)(2,1)} %copy-done.7) | copy-start | bytes 786436
  181.7 4.7 %copy-start.6 = (bf16[2,128,512]{2,1,0:T(8,128)(2,1)S(1)}, bf16[2,128,512]{2,1,0:T(8,128)(2,1)}, u32[]{:S(2)}) copy-start(bf16[2,128,512]{2,1,0:T(8,128)(2,1)} %copy-done.5) | copy-start | bytes 786436
  181.7 42.2 %all-to-all-start.3 = ((bf16[8,128,512]{2,1,0:T(8,128)(2,1)}), bf16[8,128,512]{2,1,0:T(8,128)(2,1)S(1)}, u32[]{:S(2)}, u32[]{:S(2)}) async-start(bf16[8,128,512]{2,1,0:T(8,128)(2,1)} %broadcast_in_dim.22), calls=%async_computation.3 | async-start | bytes 2097152 | tf_op jit(solution)/shard_map/all_to_all | solution.py:38
  186.5 25.2 %collective-permute-start.17 = (bf16[4,128,512]{2,1,0:T(8,128)(2,1)S(1)}, bf16[4,128,512]{2,1,0:T(8,128)(2,1)S(1)}, u32[]{:S(2)}, u32[]{:S(2)}) collective-permute-start(bf16[4,128,512]{2,1,0:T(8,128)(2,1)S(1)} %pad_maximum_fusion.2), channel_id=1, source_target_pairs={{0,4},{4,0},{1,5},{5,1},{2,6},{6,2},{3,7},{7,3},{8,12},{12,8},{9,1... | collective-permute-start | bytes 1572872 | tf_op jit(solution)/shard_map/ppermute | solution.py:431
  188.7 35.2 %copy-start.22 = (s32[4]{0:T(128)}, s32[4]{0:T(128)S(1)}, u32[]{:S(2)}) copy-start(s32[4]{0:T(128)S(1)} %and_select_fusion.peer_ref) | copy-start | bytes 52
  211.8 0.8 copy-start.16
  215.0 9.0 %copy-start.12 = (bf16[8,128,512]{2,1,0:T(8,128)(2,1)S(1)}, bf16[8,128,512]{2,1,0:T(8,128)(2,1)}, u32[]{:S(2)}) copy-start(bf16[8,128,512]{2,1,0:T(8,128)(2,1)} %token_rows_of.1) | copy-start | bytes 3145732
  223.9 1.0 copy-start.17
  224.9 5.3 %copy-start.2 = (bf16[2,32,16,512]{3,2,1,0:T(8,128)(2,1)S(1)}, bf16[2,32,16,512]{3,2,1,0:T(8,128)(2,1)}, u32[]{:S(2)}) copy-start(bf16[2,32,16,512]{3,2,1,0:T(8,128)(2,1)} %weight_rows.1) | copy-start | bytes 3145732
  225.8 62.0 %all-to-all-start.4 = ((bf16[32,24,512]{2,1,0:T(8,128)(2,1)}), bf16[32,24,512]{2,1,0:T(8,128)(2,1)S(1)}, u32[]{:S(2)}, u32[]{:S(2)}) async-start(bf16[32,24,512]{2,1,0:T(8,128)(2,1)} %pad_maximum_fusion), calls=%async_computation.4 | async-start | bytes 1572864 | tf_op jit(solution)/shard_map/all_to_all | solution.py:38
  230.1 57.8 %copy-start.19 = (f32[16,512]{1,0:T(8,128)S(1)}, f32[16,512]{1,0:T(8,128)}, u32[]{:S(2)}) copy-start(f32[16,512]{1,0:T(8,128)} %param.15) | copy-start | bytes 98308
  230.1 57.8 %copy-start.20 = (f32[16,512]{1,0:T(8,128)S(1)}, f32[16,512]{1,0:T(8,128)}, u32[]{:S(2)}) copy-start(f32[16,512]{1,0:T(8,128)} %param.14) | copy-start | bytes 98308
  230.2 26.7 %collective-permute-start.18 = (bf16[2,512,512]{2,1,0:T(8,128)(2,1)S(1)}, bf16[2,512,512]{2,1,0:T(8,128)(2,1)S(1)}, u32[]{:S(2)}, u32[]{:S(2)}) collective-permute-start(bf16[2,512,512]{2,1,0:T(8,128)(2,1)S(1)} %bitcast.78), channel_id=1, source_target_pairs={{0,1},{1,2},{2,3},{3,0},{4,5},{5,6},{6,7},{7,4},{8,9},{9,10},{10,1... | collective-permute-start | bytes 3145736 | tf_op jit(solution)/shard_map/ppermute | solution.py:393
  231.7 48.8 %collective-permute-start.19 = (bf16[2,512,512]{2,1,0:T(8,128)(2,1)S(1)}, bf16[2,512,512]{2,1,0:T(8,128)(2,1)S(1)}, u32[]{:S(2)}, u32[]{:S(2)}) collective-permute-start(bf16[2,512,512]{2,1,0:T(8,128)(2,1)S(1)} %bitcast.79), channel_id=1, source_target_pairs={{0,2},{1,3},{2,0},{3,1},{4,6},{5,7},{6,4},{7,5},{8,10},{9,11},{10,... | collective-permute-start | bytes 3145736 | tf_op jit(solution)/shard_map/ppermute | solution.py:393
  234.7 46.8 %collective-permute-start.20 = (bf16[2,512,512]{2,1,0:T(8,128)(2,1)S(1)}, bf16[2,512,512]{2,1,0:T(8,128)(2,1)}, u32[]{:S(2)}, u32[]{:S(2)}) collective-permute-start(bf16[2,512,512]{2,1,0:T(8,128)(2,1)S(1)} %bitcast.80), channel_id=1, source_target_pairs={{0,3},{1,0},{2,1},{3,2},{4,7},{5,4},{6,5},{7,6},{8,11},{9,8},{10,9... | collective-permute-start | bytes 3145736 | tf_op jit(solution)/shard_map/ppermute | solution.py:393
  256.8 24.6 %copy-start.13 = (bf16[2,512,512]{2,1,0:T(8,128)(2,1)}, bf16[2,512,512]{2,1,0:T(8,128)(2,1)S(1)}, u32[]{:S(2)}) copy-start(bf16[2,512,512]{2,1,0:T(8,128)(2,1)S(1)} %collective-permute-done.18.refs_1_) | copy-start | bytes 3145732
  280.5 1.0 copy-start.14
